TPU v7x, 32 devices: a whole 2x2x4 slice. The times are simulated.
32 devices in a mesh: items: 8 (over z, y), stream: 2 (over x), heads: 2 (over core).
Axes of the slice: x: 2, y: 2, z: 4, core: 2. Of those that a mesh axis runs over, the one named last changes fastest.
Arguments:
- hidden: bfloat16 [128, 2, 32, 768], P('items', 'stream'), may hold values from -6 to 6
- features: bfloat16 [128, 257, 1408], P('items'), may hold values from -6 to 6
- segments: int32 [128, 32], P('items'), may hold values from 0 to 2, never falling along the last dimension, each value on 1 to 16 neighbouring positions
- modes: int32 [128], P('items'), may hold values from 0 to 2
- w_qkv: bfloat16 [3, 768, 768], P(None, ('items', 'stream'), 'heads'), may hold values from -0.21875 to 0.21875
- self_bias: float32 [3, 768], replicated, may hold values from -1.5 to 1.5
- self_out: bfloat16 [768, 768], P('heads', ('items', 'stream')), may hold values from -0.625 to 0.625
- cross_q: bfloat16 [768, 768], P(('items', 'stream'), 'heads'), may hold values from -0.21875 to 0.21875
- cross_kv: bfloat16 [2, 1408, 768], P(None, ('items', 'stream'), 'heads'), may hold values from -0.15625 to 0.15625
- cross_bias: float32 [3, 768], replicated, may hold values from -1.5 to 1.5
- cross_out: bfloat16 [768, 768], P('heads', ('items', 'stream')), may hold values from -1.75 to 1.75
- gains: float32 [4, 768], replicated, may hold values from 0.25 to 1.75
- shifts: float32 [4, 768], replicated, may hold values from -1.5 to 1.5
- feat_gain: float32 [1408], replicated, may hold values from 0.25 to 1.75
- feat_shift: float32 [1408], replicated, may hold values from -1.5 to 1.5
- ffn_in: bfloat16 [2, 768, 3072], P('stream', 'items', 'heads'), may hold values from -0.21875 to 0.21875
- ffn_bias_in: float32 [2, 3072], replicated, may hold values from -1.5 to 1.5
- ffn_out: bfloat16 [2, 3072, 768], P('stream', 'heads', 'items'), may hold values from -0.15625 to 0.15625
- ffn_bias_out: float32 [2, 768], replicated, may hold values from -1.5 to 1.5
- cotangent: float32 [128, 2, 32, 768], P('items', 'stream'), may hold values from -6 to 6
Outputs:
- output: bfloat16 [128, 2, 32, 768], P('items', 'stream')
- grad_hidden: float32 [128, 2, 32, 768], P('items', 'stream')
- grad_qkv: float32 [3, 768, 768], P(None, ('items', 'stream'), 'heads')
- grad_self_bias: float32 [3, 768], replicated
- grad_self_out: float32 [768, 768], P('heads', ('items', 'stream'))
- grad_cross_q: float32 [768, 768], P(('items', 'stream'), 'heads')
- grad_cross_kv: float32 [2, 1408, 768], P(None, ('items', 'stream'), 'heads')
- grad_cross_bias: float32 [3, 768], replicated
- grad_cross_out: float32 [768, 768], P('heads', ('items', 'stream'))
- grad_gains: float32 [4, 768], replicated
- grad_shifts: float32 [4, 768], replicated
- grad_feat_gain: float32 [1408], replicated
- grad_feat_shift: float32 [1408], replicated
- grad_ffn_in: float32 [2, 768, 3072], P('stream', 'items', 'heads')
- grad_ffn_bias_in: float32 [2, 3072], replicated
- grad_ffn_out: float32 [2, 3072, 768], P('stream', 'heads', 'items')
- grad_ffn_bias_out: float32 [2, 768], replicated
Inputs may be any that keep to these rules, and one draw needn't show every extreme that they name: `segments`: each item's text row is 3 captions of consecutive tokens, each of 1 to 16 tokens. `modes`: 0: queries and text see only themselves; 1: text also sees the queries; 2: all rows see all rows.
All inputs are finite; a program needn't handle non-finite values.
Results may differ from a plain program's by a relative error of at most 0.017.
Values may be sent and summed in bfloat16 or wider, within the bound.
No kernel may reach another device: no remote copies, remote signals or barrier semaphores. Data moves between devices by JAX's collectives and lax.ppermute only.
A program may use at most 256 MiB of HBM per device.

v0:
```python
from functools import partial

import jax
import jax.numpy as jnp
from jax import lax
from jax.sharding import PartitionSpec as P

HEAD_DIM = 64


EPS = 1e-06
NEG = -1e30


def partner(shard, axis, distance):
    return lax.ppermute(shard, axis, [(i, i ^ 1 << distance) for i in range(lax.axis_size(axis))])


def standard(inputs):
    center = inputs - jnp.mean(inputs, axis=-1, keepdims=True)
    return center * lax.rsqrt(jnp.mean(center * center, axis=-1, keepdims=True) + EPS)


def normed(inputs, gain, shift):
    return standard(inputs) * gain + shift


def linear(left, weight):
    return jnp.dot(left, weight, preferred_element_type=jnp.float32)


def linear_back(gradient, weight):
    return lax.dot_general(
        gradient,
        weight,
        (((gradient.ndim - 1,), (1,)), ((), ())),
        preferred_element_type=jnp.float32,
    )


def outer_sum(left, right):
    flat_left = left.reshape(-1, left.shape[-1])
    flat_right = right.reshape(-1, right.shape[-1])
    return lax.dot_general(
        flat_left, flat_right, (((0,), (0,)), ((), ())), preferred_element_type=jnp.float32
    )


def column_sum(gradient):
    return jnp.sum(gradient, axis=(0, 1), dtype=jnp.float32)


def heads_total(partial_sum):
    return lax.psum(partial_sum, "heads")


def split_heads(inputs):
    return inputs.reshape(inputs.shape[:-1] + (inputs.shape[-1] // HEAD_DIM, HEAD_DIM))


def merge_heads(inputs):
    return inputs.reshape(inputs.shape[:-2] + (inputs.shape[-2] * inputs.shape[-1],))


def scores_of(queries, key_rows, allowed):
    scores = jnp.einsum(
        "bqhd,bkhd->bhqk",
        split_heads(queries),
        split_heads(key_rows),
        preferred_element_type=jnp.float32,
    ) * HEAD_DIM ** (-0.5)
    if allowed is not None:
        scores = jnp.where(allowed[:, None], scores, NEG)
    return scores


def attend(queries, key_rows, values, allowed):
    scores = scores_of(queries, key_rows, allowed)
    row_max = jnp.max(scores, axis=-1, keepdims=True)
    log_total = row_max + jnp.log(jnp.sum(jnp.exp(scores - row_max), axis=-1, keepdims=True))
    weights = jnp.exp(scores - log_total).astype(jnp.bfloat16)
    attended = jnp.einsum(
        "bhqk,bkhd->bqhd", weights, split_heads(values), preferred_element_type=jnp.float32
    )
    return (merge_heads(attended).astype(jnp.bfloat16), log_total)


def attend_back(queries, key_rows, values, allowed, log_total, grad_out):
    weights = jnp.exp(scores_of(queries, key_rows, allowed) - log_total)
    grad_heads = split_heads(grad_out)
    grad_weights = jnp.einsum(
        "bqhd,bkhd->bhqk", grad_heads, split_heads(values), preferred_element_type=jnp.float32
    )
    grad_values = jnp.einsum(
        "bhqk,bqhd->bkhd",
        weights.astype(jnp.bfloat16),
        grad_heads,
        preferred_element_type=jnp.float32,
    )
    row_delta = jnp.sum(grad_weights * weights, axis=-1, keepdims=True)
    grad_scores = (weights * (grad_weights - row_delta)).astype(jnp.bfloat16)
    score_scale = HEAD_DIM ** (-0.5)
    grad_queries = (
        jnp.einsum(
            "bhqk,bkhd->bqhd",
            grad_scores,
            split_heads(key_rows),
            preferred_element_type=jnp.float32,
        )
        * score_scale
    )
    grad_keys = (
        jnp.einsum(
            "bhqk,bqhd->bkhd", grad_scores, split_heads(queries), preferred_element_type=jnp.float32
        )
        * score_scale
    )
    return (merge_heads(grad_queries), merge_heads(grad_keys), merge_heads(grad_values))


def visible(stream, segments, modes):
    same_caption = segments[:, :, None] == segments[:, None, :]
    query_cols = jnp.where(stream == 0, True, modes >= 1)[:, None, None]
    text_cols = jnp.where(stream == 0, (modes == 2)[:, None, None], same_caption)
    return jnp.concatenate([jnp.broadcast_to(query_cols, same_caption.shape), text_cols], axis=2)


def feature_keys(feats, key_weight, value_weight, value_bias, feat_gain, feat_shift):
    feat_norm = normed(feats.astype(jnp.float32), feat_gain, feat_shift).astype(jnp.bfloat16)
    key_c = linear(feat_norm, key_weight).astype(jnp.bfloat16)
    value_c = (linear(feat_norm, value_weight) + value_bias).astype(jnp.bfloat16)
    return (feat_norm, key_c, value_c)


def feature_grads(feats, feat_norm, grad_keys, grad_values, key_weight, value_weight):
    key_grad = outer_sum(feat_norm, grad_keys)
    value_grad = outer_sum(feat_norm, grad_values)
    grad_norm = linear_back(grad_keys, key_weight) + linear_back(grad_values, value_weight)
    base_norm = standard(feats.astype(jnp.float32))
    gain_grad = jnp.sum(grad_norm * base_norm, axis=(0, 1))
    shift_grad = jnp.sum(grad_norm, axis=(0, 1))
    return (jnp.stack([key_grad, value_grad]), gain_grad, shift_grad, column_sum(grad_values))


def spread(piece, start, full_len):
    return lax.dynamic_update_slice_in_dim(jnp.zeros((full_len,), jnp.float32), piece, start, 0)


def body(
    hidden,
    features,
    segments,
    modes,
    w_qkv,
    self_bias,
    self_out,
    cross_q,
    cross_kv,
    cross_bias,
    cross_out,
    gains,
    shifts,
    feat_gain,
    feat_shift,
    ffn_in,
    ffn_bias_in,
    ffn_out,
    ffn_bias_out,
    cotangent,
):
    stream = lax.axis_index("stream")
    head_index = lax.axis_index("heads")
    query_side = stream == 0
    query_mask = query_side.astype(jnp.float32)
    text_mask = 1.0 - query_mask
    lead_mask = (head_index == 0).astype(jnp.float32)
    qkv_full, self_out_full, cross_q_full, cross_kv_full, cross_out_full = (
        lax.all_gather(w_qkv, ("items", "stream"), axis=1, tiled=True),
        lax.all_gather(self_out, ("items", "stream"), axis=1, tiled=True),
        lax.all_gather(cross_q, ("items", "stream"), axis=0, tiled=True),
        lax.all_gather(cross_kv, ("items", "stream"), axis=1, tiled=True),
        lax.all_gather(cross_out, ("items", "stream"), axis=1, tiled=True),
    )
    ffn_in_full, ffn_out_full = (
        lax.all_gather(ffn_in, "items", axis=1, tiled=True),
        lax.all_gather(ffn_out, "items", axis=2, tiled=True),
    )
    inner_weight = ffn_in_full[0]
    outer_weight = ffn_out_full[0]
    own_rows = hidden[:, 0]
    item_count, row_count, width = own_rows.shape
    head_cols = qkv_full.shape[2]
    head_count = head_cols // HEAD_DIM
    col_start = head_index * head_cols
    hidden_cols = inner_weight.shape[1]
    hidden_start = head_index * hidden_cols
    patch_count = features.shape[1]
    feat_width = features.shape[2]

    def my_cols(vector):
        return lax.dynamic_slice_in_dim(vector, col_start, head_cols, 0)

    bias_q = my_cols(self_bias[0])
    bias_v = my_cols(self_bias[1])
    bias_o = self_bias[2]
    bias_qc = my_cols(cross_bias[0])
    bias_vc = my_cols(cross_bias[1])
    bias_oc = cross_bias[2]
    gain_ffn = lax.dynamic_index_in_dim(gains, 2 + stream, 0, keepdims=False)
    shift_ffn = lax.dynamic_index_in_dim(shifts, 2 + stream, 0, keepdims=False)
    bias_in = lax.dynamic_slice_in_dim(
        lax.dynamic_index_in_dim(ffn_bias_in, stream, 0, keepdims=False),
        hidden_start,
        hidden_cols,
        0,
    )
    bias_out = lax.dynamic_index_in_dim(ffn_bias_out, stream, 0, keepdims=False)
    queries = (linear(own_rows, qkv_full[0]) + bias_q).astype(jnp.bfloat16)
    key_rows = linear(own_rows, qkv_full[1]).astype(jnp.bfloat16)
    values = (linear(own_rows, qkv_full[2]) + bias_v).astype(jnp.bfloat16)
    key_far, value_far = partner((key_rows, values), "stream", 0)
    all_keys = jnp.where(
        query_side,
        jnp.concatenate([key_rows, key_far], axis=1),
        jnp.concatenate([key_far, key_rows], axis=1),
    )
    all_values = jnp.where(
        query_side,
        jnp.concatenate([values, value_far], axis=1),
        jnp.concatenate([value_far, values], axis=1),
    )
    allowed = visible(stream, segments, modes)
    attended, log_total = attend(queries, all_keys, all_values, allowed)
    residual_one = (
        own_rows.astype(jnp.float32) + heads_total(linear(attended, self_out_full)) + bias_o
    )
    after_self = normed(residual_one, gains[0], shifts[0])
    after_low = after_self.astype(jnp.bfloat16)
    empty_rows = jnp.zeros((item_count, row_count, head_cols), jnp.bfloat16)
    empty_total = jnp.zeros((item_count, head_count, row_count, 1), jnp.float32)
    empty_mix = jnp.zeros((item_count, row_count, width), jnp.float32)

    def cross_front(cross_keys, cross_values):
        query_c = (linear(after_low, cross_q_full) + bias_qc).astype(jnp.bfloat16)
        attended_c, total_c = attend(query_c, cross_keys, cross_values, None)
        return (query_c, attended_c, total_c, linear(attended_c, cross_out_full))

    def front_run():
        norm_all, keys_all, values_all = feature_keys(
            features, cross_kv_full[0], cross_kv_full[1], bias_vc, feat_gain, feat_shift
        )
        return (norm_all, keys_all, values_all) + cross_front(keys_all, values_all)

    def front_skip():
        empty_feats = jnp.zeros((item_count, patch_count, feat_width), jnp.bfloat16)
        empty_keys = jnp.zeros((item_count, patch_count, head_cols), jnp.bfloat16)
        return (empty_feats, empty_keys, empty_keys, empty_rows, empty_rows, empty_total, empty_mix)

    norm_all, cross_keys, cross_values, query_c, attended_c, total_c, cross_part = lax.cond(
        query_side, front_run, front_skip
    )
    residual_two = after_self + heads_total(cross_part) + bias_oc
    after_cross = normed(residual_two, gains[1], shifts[1])
    ffn_input = jnp.where(query_side, after_cross, after_self)
    ffn_low = jnp.where(query_side, after_cross.astype(jnp.bfloat16), after_low)
    pre_act = linear(ffn_low, inner_weight) + bias_in
    activated = jax.nn.gelu(pre_act, approximate=False).astype(jnp.bfloat16)
    residual_three = ffn_input + heads_total(linear(activated, outer_weight)) + bias_out
    result_rows = normed(residual_three, gain_ffn, shift_ffn)
    output = result_rows.astype(jnp.bfloat16)[:, None]
    unused_three, norm_three_back = jax.vjp(normed, residual_three, gain_ffn, shift_ffn)
    grad_three, gain_three, shift_three = norm_three_back(cotangent[:, 0])
    grad_branch = grad_three.astype(jnp.bfloat16)
    grad_outer = outer_sum(activated, grad_branch)
    bias_out_grad = column_sum(grad_branch)
    unused_pre, gelu_back = jax.vjp(partial(jax.nn.gelu, approximate=False), pre_act)
    grad_pre = gelu_back(linear_back(grad_branch, outer_weight))[0].astype(jnp.bfloat16)
    grad_inner = outer_sum(ffn_low, grad_pre)
    bias_in_grad = column_sum(grad_pre)
    ffn_in_red, ffn_out_red = (
        lax.psum_scatter(
            grad_inner[None].astype(jnp.bfloat16), "items", scatter_dimension=1, tiled=True
        ).astype(jnp.float32),
        lax.psum_scatter(
            grad_outer[None].astype(jnp.bfloat16), "items", scatter_dimension=2, tiled=True
        ).astype(jnp.float32),
    )
    grad_ffn_input = grad_three + heads_total(linear_back(grad_pre, inner_weight))
    unused_two, norm_two_back = jax.vjp(normed, residual_two, gains[1], shifts[1])
    grad_two, gain_two, shift_two = norm_two_back(grad_ffn_input * query_mask)

    def cross_back():
        grad_mix = grad_two.astype(jnp.bfloat16)
        out_grad = outer_sum(attended_c, grad_mix)
        grad_att = linear_back(grad_mix, cross_out_full).astype(jnp.bfloat16)
        grad_qc, grad_kc, grad_vc = attend_back(
            query_c, cross_keys, cross_values, None, total_c, grad_att
        )
        grad_qc = grad_qc.astype(jnp.bfloat16)
        return (
            out_grad,
            column_sum(grad_mix),
            column_sum(grad_qc),
            outer_sum(after_low, grad_qc),
            linear_back(grad_qc, cross_q_full),
            grad_kc.astype(jnp.bfloat16),
            grad_vc.astype(jnp.bfloat16),
        )

    def back_empty():
        empty_keys = jnp.zeros((item_count, patch_count, head_cols), jnp.bfloat16)
        return (
            jnp.zeros((head_cols, width), jnp.float32),
            jnp.zeros((width,), jnp.float32),
            jnp.zeros((head_cols,), jnp.float32),
            jnp.zeros((width, head_cols), jnp.float32),
            empty_mix,
            empty_keys,
            empty_keys,
        )

    def back_run():
        pieces = cross_back()
        return pieces[:5] + feature_grads(
            features, norm_all, pieces[5], pieces[6], cross_kv_full[0], cross_kv_full[1]
        )

    def back_skip():
        pieces = back_empty()
        return pieces[:5] + (
            jnp.zeros((2, feat_width, head_cols), jnp.float32),
            jnp.zeros((feat_width,), jnp.float32),
            jnp.zeros((feat_width,), jnp.float32),
            jnp.zeros((head_cols,), jnp.float32),
        )

    (
        cross_out_grad,
        bias_oc_grad,
        bias_qc_grad,
        cross_q_grad,
        cross_part_grad,
        cross_kv_grad,
        feat_gain_grad,
        feat_shift_grad,
        bias_vc_grad,
    ) = lax.cond(query_side, back_run, back_skip)
    grad_after_self = jnp.where(query_side, grad_two + heads_total(cross_part_grad), grad_ffn_input)
    unused_one, norm_one_back = jax.vjp(normed, residual_one, gains[0], shifts[0])
    grad_one, gain_one, shift_one = norm_one_back(grad_after_self)
    grad_mix_self = grad_one.astype(jnp.bfloat16)
    self_out_grad = outer_sum(attended, grad_mix_self)
    bias_o_grad = column_sum(grad_mix_self)
    grad_attended = linear_back(grad_mix_self, self_out_full).astype(jnp.bfloat16)
    grad_q, grad_keys, grad_values = attend_back(
        queries, all_keys, all_values, allowed, log_total, grad_attended
    )
    keys_first = grad_keys[:, :row_count]
    keys_second = grad_keys[:, row_count:]
    values_first = grad_values[:, :row_count]
    values_second = grad_values[:, row_count:]
    keys_own = jnp.where(query_side, keys_first, keys_second)
    keys_away = jnp.where(query_side, keys_second, keys_first)
    values_own = jnp.where(query_side, values_first, values_second)
    values_away = jnp.where(query_side, values_second, values_first)
    keys_home, values_home = (
        partner(keys_away.astype(jnp.bfloat16), "stream", 0).astype(keys_away.dtype),
        partner(values_away.astype(jnp.bfloat16), "stream", 0).astype(values_away.dtype),
    )
    grad_kb = (keys_own + keys_home).astype(jnp.bfloat16)
    grad_vb = (values_own + values_home).astype(jnp.bfloat16)
    grad_qb = grad_q.astype(jnp.bfloat16)
    qkv_grad = jnp.stack(
        [outer_sum(own_rows, grad_qb), outer_sum(own_rows, grad_kb), outer_sum(own_rows, grad_vb)]
    )
    grad_input = grad_one + heads_total(
        linear_back(grad_qb, qkv_full[0])
        + linear_back(grad_kb, qkv_full[1])
        + linear_back(grad_vb, qkv_full[2])
    )
    qkv_red, self_out_red, cross_q_red, cross_kv_red, cross_out_red = (
        lax.psum_scatter(qkv_grad, ("items", "stream"), scatter_dimension=1, tiled=True),
        lax.psum_scatter(self_out_grad, ("items", "stream"), scatter_dimension=1, tiled=True),
        lax.psum_scatter(cross_q_grad, ("items", "stream"), scatter_dimension=0, tiled=True),
        lax.psum_scatter(cross_kv_grad, ("items", "stream"), scatter_dimension=1, tiled=True),
        lax.psum_scatter(cross_out_grad, ("items", "stream"), scatter_dimension=1, tiled=True),
    )
    self_bias_grad = jnp.stack(
        [
            spread(column_sum(grad_qb), col_start, width),
            spread(column_sum(grad_vb), col_start, width),
            lead_mask * bias_o_grad,
        ]
    )
    cross_bias_grad = jnp.stack(
        [
            spread(bias_qc_grad, col_start, width),
            spread(bias_vc_grad, col_start, width),
            lead_mask * bias_oc_grad,
        ]
    )
    gains_grad = lead_mask * jnp.stack(
        [gain_one, gain_two, query_mask * gain_three, text_mask * gain_three]
    )
    shifts_grad = lead_mask * jnp.stack(
        [shift_one, shift_two, query_mask * shift_three, text_mask * shift_three]
    )
    bias_in_full = spread(bias_in_grad, hidden_start, ffn_bias_in.shape[1])
    ffn_bias_in_grad = jnp.stack([query_mask * bias_in_full, text_mask * bias_in_full])
    ffn_bias_out_grad = lead_mask * jnp.stack(
        [query_mask * bias_out_grad, text_mask * bias_out_grad]
    )
    (
        self_bias_sum,
        cross_bias_sum,
        gains_sum,
        shifts_sum,
        feat_gain_sum,
        feat_shift_sum,
        bias_in_sum,
        bias_out_sum,
    ) = lax.psum(
        (
            self_bias_grad,
            cross_bias_grad,
            gains_grad,
            shifts_grad,
            feat_gain_grad,
            feat_shift_grad,
            ffn_bias_in_grad,
            ffn_bias_out_grad,
        ),
        ("items", "stream", "heads"),
    )
    return (
        output,
        grad_input[:, None],
        qkv_red,
        self_bias_sum,
        self_out_red,
        cross_q_red,
        cross_kv_red,
        cross_bias_sum,
        cross_out_red,
        gains_sum,
        shifts_sum,
        feat_gain_sum,
        feat_shift_sum,
        ffn_in_red,
        bias_in_sum,
        ffn_out_red,
        bias_out_sum,
    )


def solution(mesh):
    placed = (
        P("items", "stream", None, None),
        P("items", None, None),
        P("items", None),
        P("items"),
        P(None, ("items", "stream"), "heads"),
        P(),
        P("heads", ("items", "stream")),
        P(("items", "stream"), "heads"),
        P(None, ("items", "stream"), "heads"),
        P(),
        P("heads", ("items", "stream")),
        P(),
        P(),
        P(),
        P(),
        P("stream", "items", "heads"),
        P(),
        P("stream", "heads", "items"),
        P(),
        P("items", "stream", None, None),
    )
    return jax.shard_map(
        body,
        mesh=mesh,
        in_specs=placed,
        out_specs=(
            P("items", "stream", None, None),
            P("items", "stream", None, None),
            P(None, ("items", "stream"), "heads"),
            P(),
            P("heads", ("items", "stream")),
            P(("items", "stream"), "heads"),
            P(None, ("items", "stream"), "heads"),
            P(),
            P("heads", ("items", "stream")),
            P(),
            P(),
            P(),
            P(),
            P("stream", "items", "heads"),
            P(),
            P("stream", "heads", "items"),
            P(),
        ),
        check_vma=False,
    )
```

profile of v0, /device:TPU:0, one launch (start us, length us, event | category | flops | bytes accessed | tf_op | source)
XLA Modules:
  0.0 1332.8 jit_solution(16408144792853985987)
XLA Ops:
  11.6 49.4 %all_gather.22 = bf16[384,768]{0,1:T(8,128)(2,1)} all-gather(bf16[384,48]{0,1:T(8,128)(2,1)} %param.30), channel_id=1, replica_groups=mesh['items'=8,'stream'=2,'heads'=2] {'items','stream'}, dimensions={1}, use_global_device_ids=true | all-gather | bytes 626688 | tf_op jit(solution)/shard_map/all_gather | solution.py:179
  61.0 14.2 %all-gather.5.cloned.1.call-done = bf16[3,768,384]{2,1,0:T(8,128)(2,1)} async-done(((bf16[3,48,384]{2,1,0:T(8,128)(2,1)}), bf16[3,768,384]{2,1,0:T(8,128)(2,1)}) %all-gather.5.cloned.1.call-update) | async-done | bytes 1769488 | tf_op jit(solution)/shard_map/all_gather | solution.py:178
  107.7 44.6 %all_gather.24 = bf16[768,384]{1,0:T(8,128)(2,1)} all-gather(bf16[48,384]{1,0:T(8,128)(2,1)S(1)} %copy-done.63), channel_id=1, replica_groups=mesh['items'=8,'stream'=2,'heads'=2] {'items','stream'}, dimensions={0}, use_global_device_ids=true | all-gather | bytes 626688 | tf_op jit(solution)/shard_map/all_gather | solution.py:180
  152.3 43.8 %all_gather.25 = bf16[384,768]{0,1:T(8,128)(2,1)} all-gather(bf16[384,48]{0,1:T(8,128)(2,1)S(1)} %copy-done.64), channel_id=1, replica_groups=mesh['items'=8,'stream'=2,'heads'=2] {'items','stream'}, dimensions={1}, use_global_device_ids=true | all-gather | bytes 626688 | tf_op jit(solution)/shard_map/all_gather | solution.py:182
  199.4 79.9 %conditional.2 = (bf16[16,257,1408]{2,1,0:T(8,128)(2,1)}, bf16[16,257,384]{2,1,0:T(8,128)(2,1)}, bf16[16,257,384]{2,1,0:T(8,128)(2,1)}, bf16[16,32,384]{2,1,0:T(...) conditional(s32[]{:T(128)} %convert_element_type.238, () %tuple.32, ...), branch_computations={%region_5.6_spmd, %region_6.11_spmd} | conditional | flops 9780186112 | bytes 175318336 | solution.py:259
  199.5 7.5 convert_reduce_fusion.4
  207.0 8.5 fusion.28
  215.5 18.5 %fusion.31 = bf16[16,257,1408]{2,1,0:T(8,128)(2,1)S(1)} fusion(f32[1408]{0:T(1024)S(1)} %get-tuple-element.171, f32[1408]{0:T(1024)S(1)} %get-tuple-element.170, f32[16,257]{1,0:T(8,128)S(1)} %add_rsqrt_fusion.1, f32[16,257]{1,0:T(8,128)S(1)} %broadcast_multiply_fusion.1, bf16[16,257,1408]{2,0,1:T(8,128)(2,1)} %get-tuple-element.248), kind=kLoop, calls=%fused_computation.52 | loop fusion | flops 34738176 | bytes 23202944 | tf_op jit(solution)/shard_map/cond/branch_1_fun/convert_element_type | solution.py:129
  234.1 8.4 convolution_convert_fusion.2
  242.6 8.5 add_convert_fusion
  252.5 6.2 copy.120
  258.7 6.2 copy.121
  266.5 3.4 multiply_reduce_fusion.1
  271.3 4.2 fusion.36
  281.8 15.0 %all-reduce.13.cloned.1.call-done = f32[16,32,768]{2,1,0:T(8,128)} async-done(((f32[16,32,768]{2,1,0:T(8,128)}), f32[16,32,768]{2,1,0:T(8,128)}) %all-reduce.13.cloned.1.call-update) | async-done | bytes 1572880 | tf_op jit(solution)/shard_map/psum | solution.py:54
  300.7 30.0 %all-gather.9.cloned.1.call-done = bf16[1,768,1536]{2,1,0:T(8,128)(2,1)} async-done(((bf16[1,96,1536]{2,1,0:T(8,128)(2,1)}), bf16[1,768,1536]{2,1,0:T(8,128)(2,1)}) %all-gather.9.cloned.1.call-update) | async-done | bytes 2359312 | tf_op jit(solution)/shard_map/all_gather | solution.py:185
  330.7 3.9 fusion.64
  336.3 8.0 multiply_convert_fusion.3
  344.3 38.7 %all-gather.11.cloned.1.call-done = bf16[1,1536,768]{1,2,0:T(8,128)(2,1)} async-done(((bf16[1,1536,96]{1,2,0:T(8,128)(2,1)}), bf16[1,1536,768]{1,2,0:T(8,128)(2,1)}) %all-gather.11.cloned.1.call-update) | async-done | bytes 2359312 | tf_op jit(solution)/shard_map/all_gather | solution.py:186
  383.0 4.7 fusion.57
  387.8 18.9 %all-reduce.15.cloned.1.call-done = f32[16,32,768]{2,1,0:T(8,128)} async-done(((f32[16,32,768]{2,1,0:T(8,128)}), f32[16,32,768]{2,1,0:T(8,128)}) %all-reduce.15.cloned.1.call-update) | async-done | bytes 1572880 | tf_op jit(solution)/shard_map/psum | solution.py:54
  422.0 21.2 %all-reduce.17.cloned.1.call-done = f32[16,32,768]{2,1,0:T(8,128)} async-done(((f32[16,32,768]{2,1,0:T(8,128)}), f32[16,32,768]{2,1,0:T(8,128)}) %all-reduce.17.cloned.1.call-update) | async-done | bytes 1572880 | tf_op jit(solution)/shard_map/psum | solution.py:54
  448.5 118.6 %conditional.3 = (f32[384,768]{1,0:T(8,128)}, f32[768]{0:T(1024)S(1)}, f32[768,384]{0,1:T(8,128)}, f32[16,32,768]{2,1,0:T(8,128)}, f32[2,1408,384]{1,2,0:T(8,128...) conditional(s32[]{:T(128)} %convert_element_type.238, () %tuple.34, ...), branch_computations={%region_22.23_spmd, %region_23.32_spmd} | conditional | flops 19595849728 | bytes 300943392 | solution.py:347
  451.3 6.2 copy.140
  459.2 5.8 fusion.21
  465.0 6.2 copy.142
  472.4 5.9 multiply_reduce_fusion
  479.7 4.9 convert_reduce_fusion.2
  492.7 11.0 convolution_bitcast_fusion
  505.3 6.1 convolution_bitcast_fusion.1
  513.6 7.5 convert_reduce_fusion
  521.2 8.5 fusion.2
  529.7 14.0 %fusion.10 = f32[16,257,1408]{2,1,0:T(8,128)} fusion(bf16[16,257,384]{1,2,0:T(8,128)(2,1)S(1)} %bitcast.228, bf16[2,1408,384]{2,1,0:T(8,128)(2,1)} %get-tuple-element.117), kind=kOutput, calls=%fused_computation.27 | convolution fusion | flops 4446486528 | bytes 27398144 | tf_op jit(solution)/shard_map/cond/branch_1_fun/dot_general | solution.py:33
  543.7 23.1 %fusion.100 = (f32[1408]{0:T(1024)S(1)}, f32[1408]{0:T(1024)S(1)}) fusion(f32[16,257]{1,0:T(8,128)S(1)} %add_rsqrt_fusion, f32[16,257]{1,0:T(8,128)S(1)} %broadcast_multiply_fusion, bf16[16,257,1408]{2,0,1:T(8,128)(2,1)} %get-tuple-element.268, f32[16,257,1408]{2,1,0:T(8,128)} %fusion.10, bf16[16,257,384]{1,2,0:T(8,128)(2,1)} %bitcast.242, ...), kind=kOutput, calls=%fused_computation.258 | convolution fusion | flops 4487011328 | bytes 41213056 | tf_op jit(solution)/shard_map/cond/branch_1_fun/dot_general | solution.py:33
  570.2 8.6 copy.171
  578.8 4.3 copy.227
  584.3 4.5 fusion.54
  603.6 3.8 fusion.109
  617.0 3.7 fusion.108
  635.3 6.6 collective-permute-done.3
  653.0 6.3 copy.155
  672.7 5.8 copy.157
  683.3 80.6 %reduce-scatter.17.cloned.1.call-done = bf16[1,96,1536]{2,1,0:T(8,128)(2,1)} async-done(((bf16[1,768,1536]{2,1,0:T(8,128)(2,1)}), bf16[1,96,1536]{2,1,0:T(8,128)(2,1)}) %reduce-scatter.17.cloned.1.call-update) | async-done | bytes 294928 | tf_op jit(solution)/shard_map/reduce_scatter | solution.py:281
  768.6 91.5 %all-reduce.23.cloned.1.call-done = f32[3,768,384]{2,0,1:T(4,128)} async-done(((f32[3,768,384]{2,0,1:T(4,128)}), f32[3,768,384]{2,0,1:T(4,128)}) %all-reduce.23.cloned.1.call-update) | async-done | bytes 3538960
  861.8 131.6 %all-reduce.25.cloned.1.call-done = (f32[3,768]{1,0:T(4,128)}, f32[3,768]{1,0:T(4,128)}, f32[4,768]{1,0:T(4,128)}, f32[4,768]{1,0:T(4,128)}, f32[1408]{0:T(1024)...) async-done(((f32[3,768]{1,0:T(4,128)}, f32[3,768]{1,0:T(4,128)}, f32[4,768]{1,0:T(4,128)}, f32[4,768]{1,0:T(4,128)}, f32[1408]{0:T(1024)}, ...) | async-done | bytes 85008 | tf_op jit(solution)/shard_map/psum | solution.py:422
  993.4 48.7 %reduce-scatter.15.cloned.1.call-done = f32[384,48]{0,1:T(8,128)} async-done(((f32[384,768]{0,1:T(8,128)}), f32[384,48]{0,1:T(8,128)}) %reduce-scatter.15.cloned.1.call-update) | async-done | bytes 73744 | tf_op jit(solution)/shard_map/reduce_scatter | solution.py:386
  1042.1 129.3 %reduce-scatter.9.cloned.1.call-done = f32[384,48]{0,1:T(8,128)} async-done(((f32[384,768]{0,1:T(8,128)}), f32[384,48]{0,1:T(8,128)}) %reduce-scatter.9.cloned.1.call-update) | async-done | bytes 73744 | tf_op jit(solution)/shard_map/reduce_scatter | solution.py:383
  1171.3 143.1 %reduce-scatter.13.cloned.1.call-done = f32[2,88,384]{2,1,0:T(8,128)} async-done(((f32[2,1408,384]{2,1,0:T(8,128)}), f32[2,88,384]{2,1,0:T(8,128)}) %reduce-scatter.13.cloned.1.call-update) | async-done | bytes 270352 | tf_op jit(solution)/shard_map/reduce_scatter | solution.py:385
  (398 shorter events, 182.1 us)
Async XLA Ops:
  8.0 273.7 %copy-start = (f32[2,3072]{1,0:T(2,128)S(1)}, f32[2,3072]{1,0:T(2,128)}, u32[]{:S(2)}) copy-start(f32[2,3072]{1,0:T(2,128)} %param.40) | copy-start | bytes 73732
  8.0 71.3 %copy-start.14 = (bf16[16,1,32,768]{3,2,1,0:T(8,128)(2,1)S(1)}, bf16[16,1,32,768]{3,2,1,0:T(8,128)(2,1)}, u32[]{:S(2)}) copy-start(bf16[16,1,32,768]{3,2,1,0:T(8,128)(2,1)} %param.24) | copy-start | bytes 2359300
  8.0 67.2 %all-gather.5.cloned.1.call-start = ((), (), s32[]{:S(2)}) async-start(), calls=%async_computation.6 | async-start | bytes 1880064 | tf_op jit(solution)/shard_map/all_gather | solution.py:178
  8.8 187.3 %all-reduce.11.cloned.1.call-start = ((), (), s32[]{:S(2)}) async-start(), calls=%async_computation.7 | async-start | bytes 3145728 | tf_op jit(solution)/shard_map/psum | solution.py:54
  77.8 12.5 collective-permute-start.1
  81.7 15.4 %collective-permute-start = (bf16[16,32,384]{2,1,0:T(8,128)(2,1)}, bf16[16,32,384]{2,1,0:T(8,128)(2,1)}, u32[]{:S(2)}, u32[]{:S(2)}) collective-permute-start(bf16[16,32,384]{2,1,0:T(8,128)(2,1)} %fusion.68), channel_id=1, source_target_pairs={{0,2},{2,0},{1,3},{3,1},{4,6},{6,4},{5,7},{7,5},{8,10},{10,8},{9,1... | collective-permute-start | bytes 1179656 | tf_op jit(solution)/shard_map/ppermute | solution.py:16
  96.2 6.2 copy-start.4
  104.7 47.5 %copy-start.64 = (bf16[384,48]{0,1:T(8,128)(2,1)S(1)}, bf16[384,48]{0,1:T(8,128)(2,1)}, u32[]{:S(2)}) copy-start(bf16[384,48]{0,1:T(8,128)(2,1)} %param.34) | copy-start | bytes 110596
  106.5 92.9 %all-gather.7.cloned.1.call-start = ((), (), s32[]{:S(2)}) async-start(), calls=%async_computation.8 | async-start | bytes 2297856 | tf_op jit(solution)/shard_map/all_gather | solution.py:181
  107.3 189.6 %all-reduce.13.cloned.1.call-start = ((), (), s32[]{:S(2)}) async-start(), calls=%async_computation.9 | async-start | bytes 3145728 | tf_op jit(solution)/shard_map/psum | solution.py:54
  107.7 299.1 %copy-start.59 = (f32[768]{0:T(1024)}, f32[768]{0:T(1024)S(1)}, u32[]{:S(2)}) copy-start(f32[768]{0:T(1024)S(1)} %get-tuple-element.373) | copy-start | bytes 9220
  197.8 209.0 %copy-start.2 = (f32[16,32,768]{2,1,0:T(8,128)}, f32[16,32,768]{2,1,0:T(8,128)S(1)}, u32[]{:S(2)}) copy-start(f32[16,32,768]{2,1,0:T(8,128)S(1)} %get-tuple-element.332) | copy-start | bytes 4718596
  197.8 208.9 %copy-start.55 = (f32[16,32]{1,0:T(8,128)}, f32[16,32]{1,0:T(8,128)S(1)}, u32[]{:S(2)}) copy-start(f32[16,32]{1,0:T(8,128)S(1)} %broadcast_multiply_fusion.6) | copy-start | bytes 6148
  198.2 208.6 %copy-start.57 = (f32[16,32]{1,0:T(8,128)}, f32[16,32]{1,0:T(8,128)S(1)}, u32[]{:S(2)}) copy-start(f32[16,32]{1,0:T(8,128)S(1)} %fusion.95) | copy-start | bytes 6148
  215.5 18.6 %copy-start.54 = (bf16[2,1408,384]{2,1,0:T(8,128)(2,1)S(1)}, bf16[2,1408,384]{2,1,0:T(8,128)(2,1)}, u32[]{:S(2)}) copy-start(bf16[2,1408,384]{2,1,0:T(8,128)(2,1)} %get-tuple-element.101) | copy-start | bytes 6488068 | tf_op jit(solution)/shard_map/cond
  234.1 8.5 copy-start.16
  242.6 8.5 copy-start.43
  242.6 8.5 copy-start.51
  280.5 50.2 %all-gather.9.cloned.1.call-start = ((), (), s32[]{:S(2)}) async-start(), calls=%async_computation.10 | async-start | bytes 2654208 | tf_op jit(solution)/shard_map/all_gather | solution.py:185
  281.1 101.9 %all-gather.11.cloned.1.call-start = ((), (), s32[]{:S(2)}) async-start(), calls=%async_computation.11 | async-start | bytes 2654208 | tf_op jit(solution)/shard_map/all_gather | solution.py:186
  281.6 125.1 %all-reduce.15.cloned.1.call-start = ((), (), s32[]{:S(2)}) async-start(), calls=%async_computation.12 | async-start | bytes 3145728 | tf_op jit(solution)/shard_map/psum | solution.py:54
  387.8 55.5 %all-reduce.17.cloned.1.call-start = ((), (), s32[]{:S(2)}) async-start(), calls=%async_computation.13 | async-start | bytes 3145728 | tf_op jit(solution)/shard_map/psum | solution.py:54
  421.6 167.4 %all-reduce.19.cloned.1.call-start = ((), (), s32[]{:S(2)}) async-start(), calls=%async_computation.14 | async-start | bytes 3145728 | tf_op jit(solution)/shard_map/psum | solution.py:54
  459.2 5.8 copy-start.24
  465.0 6.2 copy-start.28
  471.8 6.5 slice-start
  472.4 5.9 slice-start.1
  490.2 15.0 %slice-start.4 = ((s8[11894784]{0:T(1024)(128)(4,1)}), s8[3506176]{0:T(1024)(128)(4,1)S(1)}, s32[]{:S(2)}) async-start(s8[11894784]{0:T(1024)(128)(4,1)} %bitcast.238), calls=%async_computation.28 | async-start | bytes 7012352 | tf_op jit(solution)/shard_map/cond
  492.7 11.1 copy-start.29
  492.7 11.1 copy-start.10
  492.7 11.1 copy-start.25
  492.7 12.5 slice-start.5
  492.7 12.5 slice-start.6
  567.1 113.4 %reduce-scatter.19.cloned.1.call-start = ((), (), s32[]{:S(2)}) async-start(), calls=%async_computation.21 | async-start | bytes 2654208
  583.2 180.7 %reduce-scatter.17.cloned.1.call-start = ((), (), s32[]{:S(2)}) async-start(), calls=%async_computation.20 | async-start | bytes 2654208 | tf_op jit(solution)/shard_map/reduce_scatter | solution.py:281
  588.9 176.9 %all-reduce.21.cloned.1.call-start = ((), (), s32[]{:S(2)}) async-start(), calls=%async_computation.15 | async-start | bytes 3145728 | tf_op jit(solution)/shard_map/psum | solution.py:54
  615.6 18.4 %collective-permute-start.2 = (bf16[16,32,384]{2,1,0:T(8,128)(2,1)}, bf16[16,32,384]{2,1,0:T(8,128)(2,1)}, u32[]{:S(2)}, u32[]{:S(2)}) collective-permute-start(bf16[16,32,384]{2,1,0:T(8,128)(2,1)} %select_convert_fusion.1), channel_id=1, source_target_pairs={{0,2},{2,0},{1,3},{3,1},{4,6},{6,4},{5,7},{7,5},{8,10},{10,8},{9,1... | collective-permute-start | bytes 1179656 | tf_op jit(solution)/shard_map/ppermute | solution.py:16
  630.2 11.7 copy-start.21
  630.3 11.7 copy-start.23
  630.3 11.7 collective-permute-start.3
  634.0 8.2 copy-start.46
  644.7 215.4 %all-reduce.23.cloned.1.call-start = ((), (), s32[]{:S(2)}) async-start(), calls=%async_computation.22 | async-start | bytes 9437184
  659.4 334.0 %all-reduce.25.cloned.1.call-start = ((), (), s32[]{:S(2)}) async-start(), calls=%async_computation.23 | async-start | bytes 192512 | tf_op jit(solution)/shard_map/psum | solution.py:422
  665.3 328.1 %reduce-scatter.11.cloned.1.call-start = ((), (), s32[]{:S(2)}) async-start(), calls=%async_computation.17 | async-start | bytes 1253376 | tf_op jit(solution)/shard_map/reduce_scatter | solution.py:384
  668.1 374.0 %reduce-scatter.15.cloned.1.call-start = ((), (), s32[]{:S(2)}) async-start(), calls=%async_computation.19 | async-start | bytes 1253376 | tf_op jit(solution)/shard_map/reduce_scatter | solution.py:386
  670.9 500.4 %reduce-scatter.9.cloned.1.call-start = ((), (), s32[]{:S(2)}) async-start(), calls=%async_computation.16 | async-start | bytes 1253376 | tf_op jit(solution)/shard_map/reduce_scatter | solution.py:383
  672.7 641.8 %reduce-scatter.13.cloned.1.call-start = ((), (), s32[]{:S(2)}) async-start(), calls=%async_computation.18 | async-start | bytes 4595712 | tf_op jit(solution)/shard_map/reduce_scatter | solution.py:385
  763.9 561.0 %copy-start.1 = (f32[2,3072]{1,0:T(2,128)S(1)}, f32[2,3072]{1,0:T(2,128)}, u32[]{:S(2)}) copy-start(f32[2,3072]{1,0:T(2,128)} %param.40) | copy-start | bytes 73732
  (63 other events, 166.4 us)
Sparse Core Ops, SparseCore 0:
  11.5 63.6 all-gather.4
  106.6 19.0 all-reduce.10
  128.6 64.9 all-gather.6
  280.6 16.2 all-reduce.12
  387.9 18.8 all-reduce.14
  421.7 21.5 all-reduce.16
  567.2 20.6 all-reduce.18
  644.8 21.7 all-reduce.20
  672.4 187.6 all-reduce.22
  868.1 125.2 all-reduce.24
Sparse Core Ops, SparseCore 1:
  283.1 47.5 all-gather.8
  332.8 50.2 all-gather.10
  583.3 70.0 reduce-scatter.18
  656.8 107.0 reduce-scatter.16
  769.2 143.3 reduce-scatter.10
  918.0 124.0 reduce-scatter.14
  1047.3 124.0 reduce-scatter.8
  1176.9 137.5 reduce-scatter.12
where the time goes:
time: 1340 us; the launch traced here: 1330 us
  waiting for transfers between devices  772 us (58%)
  matrix products  160 us (12%)
  blocking collectives  138 us (10%)
  local copies, waits for them, and re-layouts  129 us (10%)
  other arithmetic  109 us (8%)
  between operations  18 us (1%)
    reduce_scatter x1, waiting for transfers between devices, body(): lax.psum_scatter(cross_kv_grad, ('items', 'stream'), scatter_dimension=1,...  143 us
    psum x1, waiting for transfers between devices, body(): lax.psum((self_bias_grad, cross_bias_grad, gains_grad, shifts_grad, feat_...  132 us
    reduce_scatter x1, waiting for transfers between devices, body(): lax.psum_scatter(self_out_grad, ('items', 'stream'), scatter_dimension=1,...  129 us
    unnamed x20, waiting for transfers between devices  94.2 us
    reduce_scatter x1, waiting for transfers between devices, body(): lax.psum_scatter(grad_inner[None].astype(jnp.bfloat16), 'items', scatter_...  80.6 us
    psum x6, waiting for transfers between devices, heads_total(): return lax.psum(partial_sum, 'heads')  55.2 us
    unnamed x158, local copies, waits for them, and re-layouts  53.8 us
    dot_general x10, matrix products, linear_back(): lax.dot_general(gradient, weight, (((gradient.ndim - 1,), (1,)), ((), ())...  50.1 us
  transfers between devices with their start and end apart: 22, of which 13 were waited for; matrix products, arithmetic and copies ran while one was open for 11% of the time, Pallas kernels for 0%

commit v1 on v0

--- a/solution.py
+++ b/solution.py
@@ -1,3 +1,4 @@
+import math
 from functools import partial
 
 import jax
@@ -51,7 +52,110 @@
 
 
 def heads_total(partial_sum):
-    return lax.psum(partial_sum, "heads")
+    return partial_sum + partner(partial_sum, "heads", 0)
+
+
+def ring_of(count):
+    return list(range(0, count, 2)) + list(range(1, count, 2))[::-1]
+
+
+def ring_place(count):
+    order = ring_of(count)
+    places = [order.index(i) for i in range(count)]
+    place = jnp.asarray(places, jnp.int32)[lax.axis_index("items")]
+    return order, place
+
+
+def shift_ring(shard, order, step):
+    count = len(order)
+    return lax.ppermute(
+        shard, "items", [(order[i], order[(i + step) % count]) for i in range(count)]
+    )
+
+
+def gather_items(shard):
+    count = lax.axis_size("items")
+    order, place = ring_place(count)
+    table = jnp.asarray(order, jnp.int32)
+    rows = shard.shape[0]
+    whole = jnp.zeros((count * rows,) + shard.shape[1:], shard.dtype)
+
+    def put(whole, piece, distance):
+        start = table[(place + distance) % count] * rows
+        return lax.dynamic_update_slice_in_dim(whole, piece, start, 0)
+
+    whole = put(whole, shard, 0)
+    up = down = shard
+    for hop in range(1, count // 2 + 1):
+        up = shift_ring(up, order, 1)
+        whole = put(whole, up, count - hop)
+        if hop <= (count - 1) // 2:
+            down = shift_ring(down, order, -1)
+            whole = put(whole, down, hop)
+    return whole
+
+
+def pair_streams(shard):
+    other = partner(shard, "stream", 0)
+    first = lax.axis_index("stream") == 0
+    return jnp.where(
+        first, jnp.concatenate([shard, other], axis=0), jnp.concatenate([other, shard], axis=0)
+    )
+
+
+def scatter_items(total):
+    count = lax.axis_size("items")
+    order, place = ring_place(count)
+    table = jnp.asarray(order, jnp.int32)
+    rows = total.shape[0] // count
+
+    def piece(distance):
+        start = table[(place + distance) % count] * rows
+        return lax.dynamic_slice_in_dim(total, start, rows, 0)
+
+    far_up, far_down = count // 2, (count - 1) // 2
+    result = piece(0)
+    up = down = None
+    for hop in range(far_up, 0, -1):
+        own = piece(hop)
+        up = shift_ring((own if up is None else own + up).astype(jnp.bfloat16), order, 1).astype(jnp.float32)
+        if hop <= far_down:
+            own = piece(count - hop)
+            down = shift_ring((own if down is None else own + down).astype(jnp.bfloat16), order, -1).astype(jnp.float32)
+    return result + up + down
+
+
+def scatter_both(total):
+    count = lax.axis_size("items")
+    rows = total.shape[0] // (2 * count)
+    parts = total.reshape((count, 2, rows, total.shape[1]))
+    stream = lax.axis_index("stream")
+    keep = lax.dynamic_index_in_dim(parts, stream, 1, keepdims=False)
+    away = lax.dynamic_index_in_dim(parts, 1 - stream, 1, keepdims=False)
+    arrived = partner(away.astype(jnp.bfloat16), "stream", 0).astype(jnp.float32)
+    return scatter_items((keep + arrived).reshape(count * rows, total.shape[1]))
+
+
+def all_total(vector):
+    vector = heads_total(vector)
+    vector = vector + partner(vector, "stream", 0)
+    count = lax.axis_size("items")
+    bit = 0
+    while (1 << bit) < count:
+        vector = vector + partner(vector, "items", bit)
+        bit += 1
+    return vector
+
+
+def all_totals(arrays):
+    sizes = [math.prod(one.shape) for one in arrays]
+    packed = jnp.concatenate([one.reshape(-1) for one in arrays]).reshape(-1, 128)
+    total = all_total(packed).reshape(-1)
+    results, start = [], 0
+    for one, size in zip(arrays, sizes):
+        results.append(total[start : start + size].reshape(one.shape))
+        start += size
+    return tuple(results)
 
 
 def split_heads(inputs):
@@ -139,7 +243,7 @@
     base_norm = standard(feats.astype(jnp.float32))
     gain_grad = jnp.sum(grad_norm * base_norm, axis=(0, 1))
     shift_grad = jnp.sum(grad_norm, axis=(0, 1))
-    return (jnp.stack([key_grad, value_grad]), gain_grad, shift_grad, column_sum(grad_values))
+    return (jnp.concatenate([key_grad, value_grad], axis=1), gain_grad, shift_grad, column_sum(grad_values))
 
 
 def spread(piece, start, full_len):
@@ -174,22 +278,27 @@
     query_mask = query_side.astype(jnp.float32)
     text_mask = 1.0 - query_mask
     lead_mask = (head_index == 0).astype(jnp.float32)
-    qkv_full, self_out_full, cross_q_full, cross_kv_full, cross_out_full = (
-        lax.all_gather(w_qkv, ("items", "stream"), axis=1, tiled=True),
-        lax.all_gather(self_out, ("items", "stream"), axis=1, tiled=True),
-        lax.all_gather(cross_q, ("items", "stream"), axis=0, tiled=True),
-        lax.all_gather(cross_kv, ("items", "stream"), axis=1, tiled=True),
-        lax.all_gather(cross_out, ("items", "stream"), axis=1, tiled=True),
-    )
-    ffn_in_full, ffn_out_full = (
-        lax.all_gather(ffn_in, "items", axis=1, tiled=True),
-        lax.all_gather(ffn_out, "items", axis=2, tiled=True),
-    )
+    head_cols = w_qkv.shape[2]
+    three = [slice(i * head_cols, (i + 1) * head_cols) for i in range(3)]
+    qkv_all = gather_items(pair_streams(jnp.concatenate([w_qkv[0], w_qkv[1], w_qkv[2]], axis=1)))
+    qkv_full = [qkv_all[:, cols] for cols in three]
+    kv_all = gather_items(pair_streams(jnp.concatenate([cross_kv[0], cross_kv[1]], axis=1)))
+    cross_kv_full = [kv_all[:, cols] for cols in three[:2]]
+    rest_all = gather_items(
+        pair_streams(jnp.concatenate([self_out.T, cross_q, cross_out.T], axis=1))
+    )
+    self_out_full = rest_all[:, three[0]].T
+    cross_q_full = rest_all[:, three[1]]
+    cross_out_full = rest_all[:, three[2]].T
+    ffn_all = lax.all_gather(
+        jnp.concatenate([ffn_in[0], ffn_out[0].T], axis=1), "items", axis=0, tiled=True
+    )
+    ffn_in_full = [ffn_all[:, : ffn_in.shape[2]]]
+    ffn_out_full = [ffn_all[:, ffn_in.shape[2] :].T]
     inner_weight = ffn_in_full[0]
     outer_weight = ffn_out_full[0]
     own_rows = hidden[:, 0]
     item_count, row_count, width = own_rows.shape
-    head_cols = qkv_full.shape[2]
     head_count = head_cols // HEAD_DIM
     col_start = head_index * head_cols
     hidden_cols = inner_weight.shape[1]
@@ -271,27 +380,27 @@
     unused_three, norm_three_back = jax.vjp(normed, residual_three, gain_ffn, shift_ffn)
     grad_three, gain_three, shift_three = norm_three_back(cotangent[:, 0])
     grad_branch = grad_three.astype(jnp.bfloat16)
-    grad_outer = outer_sum(activated, grad_branch)
+    grad_outer = outer_sum(grad_branch, activated)
     bias_out_grad = column_sum(grad_branch)
     unused_pre, gelu_back = jax.vjp(partial(jax.nn.gelu, approximate=False), pre_act)
     grad_pre = gelu_back(linear_back(grad_branch, outer_weight))[0].astype(jnp.bfloat16)
     grad_inner = outer_sum(ffn_low, grad_pre)
     bias_in_grad = column_sum(grad_pre)
-    ffn_in_red, ffn_out_red = (
-        lax.psum_scatter(
-            grad_inner[None].astype(jnp.bfloat16), "items", scatter_dimension=1, tiled=True
-        ).astype(jnp.float32),
-        lax.psum_scatter(
-            grad_outer[None].astype(jnp.bfloat16), "items", scatter_dimension=2, tiled=True
-        ).astype(jnp.float32),
-    )
+    ffn_red = lax.psum_scatter(
+        jnp.concatenate([grad_inner.astype(jnp.bfloat16), grad_outer.astype(jnp.bfloat16)], axis=1),
+        "items",
+        scatter_dimension=0,
+        tiled=True,
+    ).astype(jnp.float32)
+    ffn_in_red = ffn_red[:, :hidden_cols][None]
+    ffn_out_red = ffn_red[:, hidden_cols:].T[None]
     grad_ffn_input = grad_three + heads_total(linear_back(grad_pre, inner_weight))
     unused_two, norm_two_back = jax.vjp(normed, residual_two, gains[1], shifts[1])
     grad_two, gain_two, shift_two = norm_two_back(grad_ffn_input * query_mask)
 
     def cross_back():
         grad_mix = grad_two.astype(jnp.bfloat16)
-        out_grad = outer_sum(attended_c, grad_mix)
+        out_grad = outer_sum(grad_mix, attended_c)
         grad_att = linear_back(grad_mix, cross_out_full).astype(jnp.bfloat16)
         grad_qc, grad_kc, grad_vc = attend_back(
             query_c, cross_keys, cross_values, None, total_c, grad_att
@@ -310,7 +419,7 @@
     def back_empty():
         empty_keys = jnp.zeros((item_count, patch_count, head_cols), jnp.bfloat16)
         return (
-            jnp.zeros((head_cols, width), jnp.float32),
+            jnp.zeros((width, head_cols), jnp.float32),
             jnp.zeros((width,), jnp.float32),
             jnp.zeros((head_cols,), jnp.float32),
             jnp.zeros((width, head_cols), jnp.float32),
@@ -328,7 +437,7 @@
     def back_skip():
         pieces = back_empty()
         return pieces[:5] + (
-            jnp.zeros((2, feat_width, head_cols), jnp.float32),
+            jnp.zeros((feat_width, 2 * head_cols), jnp.float32),
             jnp.zeros((feat_width,), jnp.float32),
             jnp.zeros((feat_width,), jnp.float32),
             jnp.zeros((head_cols,), jnp.float32),
@@ -349,7 +458,7 @@
     unused_one, norm_one_back = jax.vjp(normed, residual_one, gains[0], shifts[0])
     grad_one, gain_one, shift_one = norm_one_back(grad_after_self)
     grad_mix_self = grad_one.astype(jnp.bfloat16)
-    self_out_grad = outer_sum(attended, grad_mix_self)
+    self_out_grad = outer_sum(grad_mix_self, attended)
     bias_o_grad = column_sum(grad_mix_self)
     grad_attended = linear_back(grad_mix_self, self_out_full).astype(jnp.bfloat16)
     grad_q, grad_keys, grad_values = attend_back(
@@ -370,21 +479,28 @@
     grad_kb = (keys_own + keys_home).astype(jnp.bfloat16)
     grad_vb = (values_own + values_home).astype(jnp.bfloat16)
     grad_qb = grad_q.astype(jnp.bfloat16)
-    qkv_grad = jnp.stack(
-        [outer_sum(own_rows, grad_qb), outer_sum(own_rows, grad_kb), outer_sum(own_rows, grad_vb)]
+    qkv_grad = jnp.concatenate(
+        [
+            outer_sum(own_rows, grad_qb),
+            outer_sum(own_rows, grad_kb),
+            outer_sum(own_rows, grad_vb),
+            self_out_grad,
+        ],
+        axis=1,
     )
     grad_input = grad_one + heads_total(
         linear_back(grad_qb, qkv_full[0])
         + linear_back(grad_kb, qkv_full[1])
         + linear_back(grad_vb, qkv_full[2])
     )
-    qkv_red, self_out_red, cross_q_red, cross_kv_red, cross_out_red = (
-        lax.psum_scatter(qkv_grad, ("items", "stream"), scatter_dimension=1, tiled=True),
-        lax.psum_scatter(self_out_grad, ("items", "stream"), scatter_dimension=1, tiled=True),
-        lax.psum_scatter(cross_q_grad, ("items", "stream"), scatter_dimension=0, tiled=True),
-        lax.psum_scatter(cross_kv_grad, ("items", "stream"), scatter_dimension=1, tiled=True),
-        lax.psum_scatter(cross_out_grad, ("items", "stream"), scatter_dimension=1, tiled=True),
-    )
+    cross_red = scatter_both(jnp.concatenate([cross_q_grad, cross_out_grad], axis=1))
+    cross_q_red = cross_red[:, three[0]]
+    cross_out_red = cross_red[:, three[1]].T
+    kv_red = scatter_both(cross_kv_grad)
+    cross_kv_red = jnp.stack([kv_red[:, cols] for cols in three[:2]])
+    self_red = scatter_both(qkv_grad)
+    qkv_red = jnp.stack([self_red[:, cols] for cols in three])
+    self_out_red = self_red[:, 3 * head_cols :].T
     self_bias_grad = jnp.stack(
         [
             spread(column_sum(grad_qb), col_start, width),
@@ -419,7 +535,7 @@
         feat_shift_sum,
         bias_in_sum,
         bias_out_sum,
-    ) = lax.psum(
+    ) = all_totals(
         (
             self_bias_grad,
             cross_bias_grad,
@@ -429,8 +545,7 @@
             feat_shift_grad,
             ffn_bias_in_grad,
             ffn_bias_out_grad,
-        ),
-        ("items", "stream", "heads"),
+        )
     )
     return (
         output,

time: 1340 us -> 701 us (0.52)
  waiting for transfers between devices: 772 us -> 141 us
  blocking collectives: 138 us -> 0 us
  starting transfers between devices: 5.53 us -> 109 us
  between operations: 18 us -> 44 us
    reduce_scatter x5 -> x1, waiting for transfers between devices: 402 us -> 0.01 us  [body(): lax.psum_scatter(jnp.concatenate([grad_inner.astype(jnp.bfloat16), grad_o...]
    psum x7 -> x0, waiting for transfers between devices: 187 us -> none  [the longest x1 132 us: body(): lax.psum((self_bias_grad, cross_bias_grad, gains_grad, shifts_grad, feat_...]
    all_gather x3 -> x0, blocking collectives: 138 us -> none  [the longest x1 49.4 us: body(): lax.all_gather(self_out, ('items', 'stream'), axis=1, tiled=True)]
    ppermute x0 -> x42, starting transfers between devices: none -> 94.5 us  [shift_ring(): lax.ppermute(shard, 'items', [(order[i], order[(i + step) % count]) for i...]
    unnamed x20 -> x2, waiting for transfers between devices: 94.2 us -> 0.03 us
    ppermute x0 -> x42, waiting for transfers between devices: none -> 84.7 us  [shift_ring(): lax.ppermute(shard, 'items', [(order[i], order[(i + step) % count]) for i...]
    all_gather x4 -> x1, waiting for transfers between devices: 82.9 us -> 0.01 us  [body(): lax.all_gather(jnp.concatenate([ffn_in[0], ffn_out[0].T], axis=1), 'items...]
    ppermute x4 -> x21, waiting for transfers between devices: 6.62 us -> 56.5 us  [partner(): lax.ppermute(shard, axis, [(i, i ^ 1 << distance) for i in range(lax.axis...]
  transfers between devices with their start and end apart: 22 -> 65, of which waited for: 13 -> 30; matrix products, arithmetic and copies ran while one was open for 11% -> 32% of each run, Pallas kernels for 0% -> 0%
where the time goes in v1:
time: 701 us; the launch traced here: 694 us
  matrix products  149 us (21%)
  waiting for transfers between devices  141 us (20%)
  local copies, waits for them, and re-layouts  129 us (18%)
  other arithmetic  119 us (17%)
  starting transfers between devices  109 us (16%)
  between operations  44 us (6%)
    ppermute x42, starting transfers between devices, shift_ring(): lax.ppermute(shard, 'items', [(order[i], order[(i + step) % count]) for i...  94.5 us
    ppermute x42, waiting for transfers between devices, shift_ring(): lax.ppermute(shard, 'items', [(order[i], order[(i + step) % count]) for i...  84.7 us
    ppermute x21, waiting for transfers between devices, partner(): lax.ppermute(shard, axis, [(i, i ^ 1 << distance) for i in range(lax.axis...  56.5 us
    dot_general x10, matrix products, linear_back(): lax.dot_general(gradient, weight, (((gradient.ndim - 1,), (1,)), ((), ())...  55.3 us
    dot_general x10, matrix products, linear(): return jnp.dot(left, weight, preferred_element_type=jnp.float32)  32.6 us
    dot_general x10, matrix products, outer_sum(): lax.dot_general(flat_left, flat_right, (((0,), (0,)), ((), ())), preferre...  31.7 us
    unnamed x204, local copies, waits for them, and re-layouts  24 us
    reduce_sum x7, other arithmetic, standard(): center = inputs - jnp.mean(inputs, axis=-1, keepdims=True)  23.1 us
  transfers between devices with their start and end apart: 65, of which 30 were waited for; matrix products, arithmetic and copies ran while one was open for 32% of the time, Pallas kernels for 0%

profile of v1, /device:TPU:0, one launch (start us, length us, event | category | flops | bytes accessed | tf_op | source)
XLA Modules:
  0.0 694.0 jit_solution(9722004389297813924)
XLA Ops:
  42.7 5.9 collective-permute-done.1
  48.6 5.5 collective-permute-start.21
  65.0 4.2 collective-permute-done.3
  69.2 5.9 collective-permute-start.23
  78.6 11.1 %collective-permute-start.6 = (bf16[96,1152]{1,0:T(8,128)(2,1)S(1)}, bf16[96,1152]{1,0:T(8,128)(2,1)S(1)}, u32[]{:S(2)}, u32[]{:S(2)}) collective-permute-start(bf16[96,1152]{1,0:T(8,128)(2,1)S(1)} %collective-permute-done.4), channel_id=1, source_target_pairs={{0,4},{8,0},{16,8},{24,16},{28,24},{20,28},{12,20},{4,12},{1,5},{9... | collective-permute-start | bytes 663560 | tf_op jit(solution)/shard_map/ppermute | solution.py:71
  89.9 9.8 %collective-permute-done.5 = bf16[96,1152]{1,0:T(8,128)(2,1)S(1)} collective-permute-done((bf16[96,1152]{1,0:T(8,128)(2,1)S(1)}, bf16[96,1152]{1,0:T(8,128)(2,1)S(1)}, u32[]{:S(2)}, u32[]{:S(2)}) %collective-permute-start.5) | collective-permute-done | bytes 221216 | tf_op jit(solution)/shard_map/ppermute | solution.py:71
  99.7 20.4 %collective-permute-start.16 = (bf16[96,1152]{1,0:T(8,128)(2,1)S(1)}, bf16[96,1152]{1,0:T(8,128)(2,1)S(1)}, u32[]{:S(2)}, u32[]{:S(2)}) collective-permute-start(bf16[96,1152]{1,0:T(8,128)(2,1)S(1)} %collective-permute-done.14), channel_id=1, source_target_pairs={{0,4},{8,0},{16,8},{24,16},{28,24},{20,28},{12,20},{4,12},{1,5},{9... | collective-permute-start | bytes 663560 | tf_op jit(solution)/shard_map/ppermute | solution.py:71
  120.2 4.7 collective-permute-start.7
  128.9 4.5 collective-permute-done.7
  148.0 6.2 collective-permute-done.8
  158.1 4.5 maximum_select_fusion
  174.8 3.9 collective-permute-done.24
  180.8 6.2 collective-permute-done.26
  190.7 71.3 %conditional.2 = (bf16[16,257,1408]{2,1,0:T(8,128)(2,1)}, bf16[16,257,384]{2,1,0:T(8,128)(2,1)}, bf16[16,257,384]{2,1,0:T(8,128)(2,1)}, bf16[16,32,384]{2,1,0:T(...) conditional(s32[]{:T(128)} %convert_element_type.379, () %tuple.30, ...), branch_computations={%region_4.5_spmd, %region_5.10_spmd.clone.clone} | conditional | flops 9780186112 | bytes 183386976 | solution.py:368
  192.0 7.7 %convert_reduce_fusion.4 = f32[16,257]{1,0:T(8,128)S(1)} fusion(bf16[16,257,1408]{2,0,1:T(8,128)(2,1)} %get-tuple-element.264), kind=kLoop, calls=%fused_computation.44 | loop fusion | flops 11575280 | bytes 11595840 | tf_op jit(solution)/shard_map/cond/branch_1_fun/reduce_sum | solution.py:21
  199.7 8.5 %fusion.26 = f32[16,257]{1,0:T(8,128)S(1)} fusion(f32[16,257]{1,0:T(8,128)S(1)} %broadcast_multiply_fusion.1, bf16[16,257,1408]{2,0,1:T(8,128)(2,1)} %get-tuple-element.264), kind=kLoop, calls=%fused_computation.47 | loop fusion | flops 23154672 | bytes 11612288 | tf_op jit(solution)/shard_map/cond/branch_1_fun/reduce_sum | solution.py:22
  208.8 9.0 %fusion.29 = bf16[16,257,1408]{2,1,0:T(8,128)(2,1)S(1)} fusion(f32[1408]{0:T(1024)S(1)} %get-tuple-element.266, f32[1408]{0:T(1024)S(1)} %get-tuple-element.265, f32[16,257]{1,0:T(8,128)S(1)} %add_rsqrt_fusion.1, f32[16,257]{1,0:T(8,128)S(1)} %broadcast_multiply_fusion.1, bf16[16,257,1408]{2,0,1:T(8,128)(2,1)} %get-tuple-element.264), kind=kLoop, calls=%fused_computation.50 | loop fusion | flops 34738176 | bytes 23202944 | tf_op jit(solution)/shard_map/cond/branch_1_fun/convert_element_type | solution.py:233
  217.8 8.4 %add_convert_fusion = bf16[16,257,384]{2,1,0:T(8,128)(2,1)} fusion(f32[384]{0:T(512)S(1)} %get-tuple-element.334, bf16[16,257,1408]{2,1,0:T(8,128)(2,1)S(1)} %fusion.29, bf16[1408,384]{1,0:T(8,128)(2,1)S(1)} %copy-done.66), kind=kOutput, calls=%fused_computation.51 | convolution fusion | flops 4449644544 | bytes 15820288 | tf_op jit(solution)/shard_map/cond/branch_1_fun/dot_general | solution.py:30
  226.2 8.4 %convolution_convert_fusion.2 = bf16[16,257,384]{2,1,0:T(8,128)(2,1)} fusion(bf16[16,257,1408]{2,1,0:T(8,128)(2,1)S(1)} %fusion.29, bf16[1408,384]{1,0:T(8,128)(2,1)S(1)} %copy-done.39), kind=kOutput, calls=%fused_computation.58 | convolution fusion | flops 4448065536 | bytes 15818752 | tf_op jit(solution)/shard_map/cond/branch_1_fun/dot_general | solution.py:30
  234.7 6.2 copy.146
  246.5 6.2 copy.145
  252.7 5.6 fusion.34
  270.0 3.9 fusion.54
  274.0 7.8 %multiply_convert_fusion.3 = (bf16[16,32,1536]{2,1,0:T(8,128)(2,1)S(1)}, f32[16,32,1536]{2,1,0:T(8,128)}) fusion(f32[16,32,1536]{2,1,0:T(8,128)S(1)} %get-tuple-element.406, u16[32,1536]{1,0:T(8,128)(2,1)S(1)} %get-tuple-element.295, u16[32,1536]{1,0:T(8,128)(2,1)S(1)} %get-tuple-element.294), kind=kLoop, calls=%fused_computation.90 | loop fusion | flops 55050240 | bytes 8060928 | tf_op jit(solution)/shard_map/convert_element_type | solution.py:376
  315.0 4.7 fusion.50
  331.9 125.1 %conditional.3 = (f32[768,384]{1,0:T(8,128)}, f32[768]{0:T(1024)S(1)}, f32[16,32,768]{2,1,0:T(8,128)}, f32[1408]{0:T(1024)S(1)}, f32[1408]{0:T(1024)S(1)}, /*ind...) conditional(s32[]{:T(128)} %convert_element_type.379, () %tuple.32, ...), branch_computations={%region_18.19_spmd, %region_19.28_spmd} | conditional | flops 19595849728 | bytes 325998976 | solution.py:456
  332.2 7.5 %convert_reduce_fusion = f32[16,257]{1,0:T(8,128)S(1)} fusion(bf16[16,257,1408]{2,0,1:T(8,128)(2,1)} %get-tuple-element.244), kind=kLoop, calls=%fused_computation.1 | loop fusion | flops 11575280 | bytes 11595840 | tf_op jit(solution)/shard_map/cond/branch_1_fun/reduce_sum | solution.py:21
  339.7 8.5 %fusion.2 = f32[16,257]{1,0:T(8,128)S(1)} fusion(f32[16,257]{1,0:T(8,128)S(1)} %broadcast_multiply_fusion, bf16[16,257,1408]{2,0,1:T(8,128)(2,1)} %get-tuple-element.244), kind=kLoop, calls=%fused_computation.4 | loop fusion | flops 23154672 | bytes 11612288 | tf_op jit(solution)/shard_map/cond/branch_1_fun/reduce_sum | solution.py:22
  355.3 6.2 copy.117
  361.5 6.2 copy.115
  376.9 3.8 convert_reduce_fusion.1
  392.5 11.2 %convolution_bitcast_fusion.1 = f32[1408,384]{0,1:T(8,128)S(1)} fusion(bf16[16,257,384]{1,2,0:T(8,128)(2,1)S(1)} %bitcast.301, bf16[16,257,1408]{2,1,0:T(8,128)(2,1)} %get-tuple-element.71), kind=kOutput, calls=%fused_computation.16 | convolution fusion | flops 4446486528 | bytes 16900096 | tf_op jit(solution)/shard_map/cond/branch_1_fun/dot_general | solution.py:45
  403.8 6.1 convolution_bitcast_fusion
  412.2 5.9 copy.104
  418.1 15.5 %fusion.10 = f32[16,257,1408]{2,1,0:T(8,128)} fusion(bf16[16,257,384]{1,2,0:T(8,128)(2,1)} %bitcast.302, bf16[1408,384]{1,0:T(8,128)(2,1)S(1)} %copy-done.40), kind=kOutput, calls=%fused_computation.27 | convolution fusion | flops 4446486528 | bytes 27398144 | tf_op jit(solution)/shard_map/cond/branch_1_fun/dot_general | solution.py:34
  433.6 23.2 %fusion.98 = (f32[1408]{0:T(1024)S(1)}, f32[1408]{0:T(1024)S(1)}) fusion(f32[16,257]{1,0:T(8,128)S(1)} %copy-done.87, f32[16,257]{1,0:T(8,128)S(1)} %broadcast_multiply_fusion, bf16[16,257,1408]{2,0,1:T(8,128)(2,1)} %get-tuple-element.244, f32[16,257,1408]{2,1,0:T(8,128)} %fusion.10, bf16[16,257,384]{1,2,0:T(8,128)(2,1)} %bitcast.329, ...), kind=kOutput, calls=%fused_computation.347 | convolution fusion | flops 4487011328 | bytes 39021696 | tf_op jit(solution)/shard_map/cond/branch_1_fun/dot_general | solution.py:34
  467.2 9.5 %collective-permute-done.47 = bf16[8,48,768]{2,1,0:T(8,128)(2,1)S(1)} collective-permute-done((bf16[8,48,768]{2,1,0:T(8,128)(2,1)S(1)}, bf16[8,48,768]{2,1,0:T(8,128)(2,1)S(1)}, u32[]{:S(2)}, u32[]{:S(2)}) %collective-permute-start.47) | collective-permute-done | bytes 589856 | tf_op jit(solution)/shard_map/ppermute | solution.py:17
  478.8 3.8 collective-permute-done.48
  493.7 4.5 collective-permute-done.50
  512.1 4.0 collective-permute-start.57
  518.5 5.1 collective-permute-done.57
  524.4 7.6 %collective-permute-done.58 = bf16[88,768]{1,0:T(8,128)(2,1)S(1)} collective-permute-done((bf16[88,768]{1,0:T(8,128)(2,1)S(1)}, bf16[88,768]{1,0:T(8,128)(2,1)S(1)}, u32[]{:S(2)}, u32[]{:S(2)}) %collective-permute-start.58) | collective-permute-done | bytes 135200 | tf_op jit(solution)/shard_map/ppermute | solution.py:71
  581.9 4.3 collective-permute-done.62
  597.6 6.1 copy.130
  609.5 26.7 %collective-permute-done.43 = f32[166,128]{1,0:T(8,128)S(1)} collective-permute-done((f32[166,128]{1,0:T(8,128)S(1)}, f32[166,128]{1,0:T(8,128)S(1)}, u32[]{:S(2)}, u32[]{:S(2)}) %collective-permute-start.43) | collective-permute-done | bytes 85024 | tf_op jit(solution)/shard_map/ppermute | solution.py:17
  637.8 3.8 collective-permute-done.44
  642.3 3.9 collective-permute-done.45
  648.1 3.9 collective-permute-done.46
  (611 shorter events, 301.8 us)
Async XLA Ops:
  7.3 262.7 %all-gather.2.cloned.1.call-start = ((), (), s32[]{:S(2)}) async-start(), calls=%async_computation.1 | async-start | bytes 5308416 | tf_op jit(solution)/shard_map/all_gather | solution.py:293
  8.2 28.1 %collective-permute-start = (bf16[48,1152]{1,0:T(8,128)(2,1)S(1)}, bf16[48,1152]{1,0:T(8,128)(2,1)S(1)}, u32[]{:S(2)}, u32[]{:S(2)}) collective-permute-start(bf16[48,1152]{1,0:T(8,128)(2,1)S(1)} %pad_maximum_fusion.8), channel_id=1, source_target_pairs={{0,2},{2,0},{1,3},{3,1},{4,6},{6,4},{5,7},{7,5},{8,10},{10,8},{9,1... | collective-permute-start | bytes 331784 | tf_op jit(solution)/shard_map/ppermute | solution.py:17
  12.0 26.5 %collective-permute-start.10 = (bf16[48,1152]{1,0:T(8,128)(2,1)S(1)}, bf16[48,1152]{1,0:T(8,128)(2,1)S(1)}, u32[]{:S(2)}, u32[]{:S(2)}) collective-permute-start(bf16[48,1152]{1,0:T(8,128)(2,1)S(1)} %pad_maximum_fusion.9), channel_id=1, source_target_pairs={{0,2},{2,0},{1,3},{3,1},{4,6},{6,4},{5,7},{7,5},{8,10},{10,8},{9,1... | collective-permute-start | bytes 331784 | tf_op jit(solution)/shard_map/ppermute | solution.py:17
  13.1 27.8 %collective-permute-start.19 = (bf16[88,768]{1,0:T(8,128)(2,1)S(1)}, bf16[88,768]{1,0:T(8,128)(2,1)S(1)}, u32[]{:S(2)}, u32[]{:S(2)}) collective-permute-start(bf16[88,768]{1,0:T(8,128)(2,1)S(1)} %pad_maximum_fusion.7), channel_id=1, source_target_pairs={{0,2},{2,0},{1,3},{3,1},{4,6},{6,4},{5,7},{7,5},{8,10},{10,8},{9,1... | collective-permute-start | bytes 405512 | tf_op jit(solution)/shard_map/ppermute | solution.py:17
  17.1 667.6 %reduce-scatter.2.cloned.1.call-start = ((), (), s32[]{:S(2)}) async-start(), calls=%async_computation.2 | async-start | bytes 5308416 | tf_op jit(solution)/shard_map/reduce_scatter | solution.py:389
  36.5 12.2 %collective-permute-start.1 = (bf16[96,1152]{1,0:T(8,128)(2,1)S(1)}, bf16[96,1152]{1,0:T(8,128)(2,1)S(1)}, u32[]{:S(2)}, u32[]{:S(2)}) collective-permute-start(bf16[96,1152]{1,0:T(8,128)(2,1)S(1)} %get-tuple-element.330), channel_id=1, source_target_pairs={{0,8},{8,16},{16,24},{24,28},{28,20},{20,12},{12,4},{4,0},{1,9},{9... | collective-permute-start | bytes 663560 | tf_op jit(solution)/shard_map/ppermute | solution.py:71
  38.1 16.1 %collective-permute-start.2 = (bf16[96,1152]{1,0:T(8,128)(2,1)S(1)}, bf16[96,1152]{1,0:T(8,128)(2,1)S(1)}, u32[]{:S(2)}, u32[]{:S(2)}) collective-permute-start(bf16[96,1152]{1,0:T(8,128)(2,1)S(1)} %get-tuple-element.330), channel_id=1, source_target_pairs={{0,4},{8,0},{16,8},{24,16},{28,24},{20,28},{12,20},{4,12},{1,5},{9... | collective-permute-start | bytes 663560 | tf_op jit(solution)/shard_map/ppermute | solution.py:71
  38.8 16.8 %collective-permute-start.11 = (bf16[96,1152]{1,0:T(8,128)(2,1)S(1)}, bf16[96,1152]{1,0:T(8,128)(2,1)S(1)}, u32[]{:S(2)}, u32[]{:S(2)}) collective-permute-start(bf16[96,1152]{1,0:T(8,128)(2,1)S(1)} %get-tuple-element.328), channel_id=1, source_target_pairs={{0,8},{8,16},{16,24},{24,28},{28,20},{20,12},{12,4},{4,0},{1,9},{9... | collective-permute-start | bytes 663560 | tf_op jit(solution)/shard_map/ppermute | solution.py:71
  40.4 18.5 %collective-permute-start.12 = (bf16[96,1152]{1,0:T(8,128)(2,1)S(1)}, bf16[96,1152]{1,0:T(8,128)(2,1)S(1)}, u32[]{:S(2)}, u32[]{:S(2)}) collective-permute-start(bf16[96,1152]{1,0:T(8,128)(2,1)S(1)} %get-tuple-element.328), channel_id=1, source_target_pairs={{0,4},{8,0},{16,8},{24,16},{28,24},{20,28},{12,20},{4,12},{1,5},{9... | collective-permute-start | bytes 663560 | tf_op jit(solution)/shard_map/ppermute | solution.py:71
  41.1 20.3 %collective-permute-start.20 = (bf16[176,768]{1,0:T(8,128)(2,1)S(1)}, bf16[176,768]{1,0:T(8,128)(2,1)}, u32[]{:S(2)}, u32[]{:S(2)}) collective-permute-start(bf16[176,768]{1,0:T(8,128)(2,1)S(1)} %get-tuple-element.324), channel_id=1, source_target_pairs={{0,8},{8,16},{16,24},{24,28},{28,20},{20,12},{12,4},{4,0},{1,9},{9... | collective-permute-start | bytes 811016 | tf_op jit(solution)/shard_map/ppermute | solution.py:71
  48.6 16.1 %collective-permute-start.21 = (bf16[176,768]{1,0:T(8,128)(2,1)S(1)}, bf16[176,768]{1,0:T(8,128)(2,1)}, u32[]{:S(2)}, u32[]{:S(2)}) collective-permute-start(bf16[176,768]{1,0:T(8,128)(2,1)S(1)} %get-tuple-element.324), channel_id=1, source_target_pairs={{0,4},{8,0},{16,8},{24,16},{28,24},{20,28},{12,20},{4,12},{1,5},{9... | collective-permute-start | bytes 811016 | tf_op jit(solution)/shard_map/ppermute | solution.py:71
  54.2 15.0 %collective-permute-start.3 = (bf16[96,1152]{1,0:T(8,128)(2,1)S(1)}, bf16[96,1152]{1,0:T(8,128)(2,1)S(1)}, u32[]{:S(2)}, u32[]{:S(2)}) collective-permute-start(bf16[96,1152]{1,0:T(8,128)(2,1)S(1)} %collective-permute-done.1), channel_id=1, source_target_pairs={{0,8},{8,16},{16,24},{24,28},{28,20},{20,12},{12,4},{4,0},{1,9},{9... | collective-permute-start | bytes 663560 | tf_op jit(solution)/shard_map/ppermute | solution.py:71
  55.5 19.5 %collective-permute-start.4 = (bf16[96,1152]{1,0:T(8,128)(2,1)S(1)}, bf16[96,1152]{1,0:T(8,128)(2,1)S(1)}, u32[]{:S(2)}, u32[]{:S(2)}) collective-permute-start(bf16[96,1152]{1,0:T(8,128)(2,1)S(1)} %collective-permute-done.2), channel_id=1, source_target_pairs={{0,4},{8,0},{16,8},{24,16},{28,24},{20,28},{12,20},{4,12},{1,5},{9... | collective-permute-start | bytes 663560 | tf_op jit(solution)/shard_map/ppermute | solution.py:71
  58.9 19.7 %collective-permute-start.13 = (bf16[96,1152]{1,0:T(8,128)(2,1)S(1)}, bf16[96,1152]{1,0:T(8,128)(2,1)S(1)}, u32[]{:S(2)}, u32[]{:S(2)}) collective-permute-start(bf16[96,1152]{1,0:T(8,128)(2,1)S(1)} %collective-permute-done.11), channel_id=1, source_target_pairs={{0,8},{8,16},{16,24},{24,28},{28,20},{20,12},{12,4},{4,0},{1,9},{9... | collective-permute-start | bytes 663560 | tf_op jit(solution)/shard_map/ppermute | solution.py:71
  61.3 28.5 %collective-permute-start.14 = (bf16[96,1152]{1,0:T(8,128)(2,1)S(1)}, bf16[96,1152]{1,0:T(8,128)(2,1)S(1)}, u32[]{:S(2)}, u32[]{:S(2)}) collective-permute-start(bf16[96,1152]{1,0:T(8,128)(2,1)S(1)} %collective-permute-done.12), channel_id=1, source_target_pairs={{0,4},{8,0},{16,8},{24,16},{28,24},{20,28},{12,20},{4,12},{1,5},{9... | collective-permute-start | bytes 663560 | tf_op jit(solution)/shard_map/ppermute | solution.py:71
  64.8 104.9 %collective-permute-start.22 = (bf16[176,768]{1,0:T(8,128)(2,1)}, bf16[176,768]{1,0:T(8,128)(2,1)}, u32[]{:S(2)}, u32[]{:S(2)}) collective-permute-start(bf16[176,768]{1,0:T(8,128)(2,1)} %collective-permute-done.20), channel_id=1, source_target_pairs={{0,8},{8,16},{16,24},{24,28},{28,20},{20,12},{12,4},{4,0},{1,9},{9... | collective-permute-start | bytes 811016 | tf_op jit(solution)/shard_map/ppermute | solution.py:71
  69.2 101.6 %collective-permute-start.23 = (bf16[176,768]{1,0:T(8,128)(2,1)}, bf16[176,768]{1,0:T(8,128)(2,1)}, u32[]{:S(2)}, u32[]{:S(2)}) collective-permute-start(bf16[176,768]{1,0:T(8,128)(2,1)} %collective-permute-done.21), channel_id=1, source_target_pairs={{0,4},{8,0},{16,8},{24,16},{28,24},{20,28},{12,20},{4,12},{1,5},{9... | collective-permute-start | bytes 811016 | tf_op jit(solution)/shard_map/ppermute | solution.py:71
  75.1 24.6 %collective-permute-start.5 = (bf16[96,1152]{1,0:T(8,128)(2,1)S(1)}, bf16[96,1152]{1,0:T(8,128)(2,1)S(1)}, u32[]{:S(2)}, u32[]{:S(2)}) collective-permute-start(bf16[96,1152]{1,0:T(8,128)(2,1)S(1)} %collective-permute-done.3), channel_id=1, source_target_pairs={{0,8},{8,16},{16,24},{24,28},{28,20},{20,12},{12,4},{4,0},{1,9},{9... | collective-permute-start | bytes 663560 | tf_op jit(solution)/shard_map/ppermute | solution.py:71
  78.6 47.2 %collective-permute-start.6 = (bf16[96,1152]{1,0:T(8,128)(2,1)S(1)}, bf16[96,1152]{1,0:T(8,128)(2,1)S(1)}, u32[]{:S(2)}, u32[]{:S(2)}) collective-permute-start(bf16[96,1152]{1,0:T(8,128)(2,1)S(1)} %collective-permute-done.4), channel_id=1, source_target_pairs={{0,4},{8,0},{16,8},{24,16},{28,24},{20,28},{12,20},{4,12},{1,5},{9... | collective-permute-start | bytes 663560 | tf_op jit(solution)/shard_map/ppermute | solution.py:71
  89.8 30.3 %collective-permute-start.15 = (bf16[96,1152]{1,0:T(8,128)(2,1)S(1)}, bf16[96,1152]{1,0:T(8,128)(2,1)}, u32[]{:S(2)}, u32[]{:S(2)}) collective-permute-start(bf16[96,1152]{1,0:T(8,128)(2,1)S(1)} %collective-permute-done.13), channel_id=1, source_target_pairs={{0,8},{8,16},{16,24},{24,28},{28,20},{20,12},{12,4},{4,0},{1,9},{9... | collective-permute-start | bytes 663560 | tf_op jit(solution)/shard_map/ppermute | solution.py:71
  99.7 29.1 %collective-permute-start.16 = (bf16[96,1152]{1,0:T(8,128)(2,1)S(1)}, bf16[96,1152]{1,0:T(8,128)(2,1)S(1)}, u32[]{:S(2)}, u32[]{:S(2)}) collective-permute-start(bf16[96,1152]{1,0:T(8,128)(2,1)S(1)} %collective-permute-done.14), channel_id=1, source_target_pairs={{0,4},{8,0},{16,8},{24,16},{28,24},{20,28},{12,20},{4,12},{1,5},{9... | collective-permute-start | bytes 663560 | tf_op jit(solution)/shard_map/ppermute | solution.py:71
  120.2 13.3 %collective-permute-start.7 = (bf16[96,1152]{1,0:T(8,128)(2,1)S(1)}, bf16[96,1152]{1,0:T(8,128)(2,1)S(1)}, u32[]{:S(2)}, u32[]{:S(2)}) collective-permute-start(bf16[96,1152]{1,0:T(8,128)(2,1)S(1)} %collective-permute-done.5), channel_id=1, source_target_pairs={{0,8},{8,16},{16,24},{24,28},{28,20},{20,12},{12,4},{4,0},{1,9},{9... | collective-permute-start | bytes 663560 | tf_op jit(solution)/shard_map/ppermute | solution.py:71
  125.8 20.5 %collective-permute-start.17 = (bf16[96,1152]{1,0:T(8,128)(2,1)}, bf16[96,1152]{1,0:T(8,128)(2,1)}, u32[]{:S(2)}, u32[]{:S(2)}) collective-permute-start(bf16[96,1152]{1,0:T(8,128)(2,1)} %collective-permute-done.15), channel_id=1, source_target_pairs={{0,8},{8,16},{16,24},{24,28},{28,20},{20,12},{12,4},{4,0},{1,9},{9... | collective-permute-start | bytes 663560 | tf_op jit(solution)/shard_map/ppermute | solution.py:71
  136.1 20.5 %collective-permute-start.9 = (bf16[16,32,384]{2,1,0:T(8,128)(2,1)}, bf16[16,32,384]{2,1,0:T(8,128)(2,1)S(1)}, u32[]{:S(2)}, u32[]{:S(2)}) collective-permute-start(bf16[16,32,384]{2,1,0:T(8,128)(2,1)} %fusion.62), channel_id=1, source_target_pairs={{0,2},{2,0},{1,3},{3,1},{4,6},{6,4},{5,7},{7,5},{8,10},{10,8},{9,1... | collective-permute-start | bytes 1179656 | tf_op jit(solution)/shard_map/ppermute | solution.py:17
  139.3 14.9 %collective-permute-start.8 = (bf16[16,32,384]{2,1,0:T(8,128)(2,1)}, bf16[16,32,384]{2,1,0:T(8,128)(2,1)}, u32[]{:S(2)}, u32[]{:S(2)}) collective-permute-start(bf16[16,32,384]{2,1,0:T(8,128)(2,1)} %fusion.61), channel_id=1, source_target_pairs={{0,2},{2,0},{1,3},{3,1},{4,6},{6,4},{5,7},{7,5},{8,10},{10,8},{9,1... | collective-permute-start | bytes 1179656 | tf_op jit(solution)/shard_map/ppermute | solution.py:17
  168.5 20.0 %collective-permute-start.18 = (f32[16,32,768]{2,1,0:T(8,128)S(1)}, f32[16,32,768]{2,1,0:T(8,128)S(1)}, u32[]{:S(2)}, u32[]{:S(2)}) collective-permute-start(f32[16,32,768]{2,1,0:T(8,128)S(1)} %fusion.86), channel_id=1, source_target_pairs={{0,1},{1,0},{2,3},{3,2},{4,5},{5,4},{6,7},{7,6},{8,9},{9,8},{10,11... | collective-permute-start | bytes 4718600 | tf_op jit(solution)/shard_map/ppermute | solution.py:17
  169.7 9.0 %collective-permute-start.24 = (bf16[176,768]{1,0:T(8,128)(2,1)}, bf16[176,768]{1,0:T(8,128)(2,1)S(1)}, u32[]{:S(2)}, u32[]{:S(2)}) collective-permute-start(bf16[176,768]{1,0:T(8,128)(2,1)} %collective-permute-done.22), channel_id=1, source_target_pairs={{0,8},{8,16},{16,24},{24,28},{28,20},{20,12},{12,4},{4,0},{1,9},{9... | collective-permute-start | bytes 811016 | tf_op jit(solution)/shard_map/ppermute | solution.py:71
  170.8 9.0 %collective-permute-start.25 = (bf16[176,768]{1,0:T(8,128)(2,1)}, bf16[176,768]{1,0:T(8,128)(2,1)S(1)}, u32[]{:S(2)}, u32[]{:S(2)}) collective-permute-start(bf16[176,768]{1,0:T(8,128)(2,1)} %collective-permute-done.23), channel_id=1, source_target_pairs={{0,4},{8,0},{16,8},{24,16},{28,24},{20,28},{12,20},{4,12},{1,5},{9... | collective-permute-start | bytes 811016 | tf_op jit(solution)/shard_map/ppermute | solution.py:71
  284.4 13.4 %collective-permute-start.28 = (f32[16,32,768]{2,1,0:T(8,128)}, f32[16,32,768]{2,1,0:T(8,128)}, u32[]{:S(2)}, u32[]{:S(2)}) collective-permute-start(f32[16,32,768]{2,1,0:T(8,128)} %fusion.51), channel_id=1, source_target_pairs={{0,1},{1,0},{2,3},{3,2},{4,5},{5,4},{6,7},{7,6},{8,9},{9,8},{10,11... | collective-permute-start | bytes 4718600 | tf_op jit(solution)/shard_map/ppermute | solution.py:17
  460.5 16.3 %collective-permute-start.47 = (bf16[8,48,768]{2,1,0:T(8,128)(2,1)S(1)}, bf16[8,48,768]{2,1,0:T(8,128)(2,1)S(1)}, u32[]{:S(2)}, u32[]{:S(2)}) collective-permute-start(bf16[8,48,768]{2,1,0:T(8,128)(2,1)S(1)} %fusion.77), channel_id=1, source_target_pairs={{0,2},{2,0},{1,3},{3,1},{4,6},{6,4},{5,7},{7,5},{8,10},{10,8},{9,1... | collective-permute-start | bytes 1769480 | tf_op jit(solution)/shard_map/ppermute | solution.py:17
  465.2 38.7 %collective-permute-start.55 = (bf16[8,88,768]{2,1,0:T(8,128)(2,1)}, bf16[8,88,768]{2,1,0:T(8,128)(2,1)}, u32[]{:S(2)}, u32[]{:S(2)}) collective-permute-start(bf16[8,88,768]{2,1,0:T(8,128)(2,1)} %fusion.70), channel_id=1, source_target_pairs={{0,2},{2,0},{1,3},{3,1},{4,6},{6,4},{5,7},{7,5},{8,10},{10,8},{9,1... | collective-permute-start | bytes 3244040 | tf_op jit(solution)/shard_map/ppermute | solution.py:17
  482.6 8.5 %collective-permute-start.49 = (bf16[48,768]{1,0:T(8,128)(2,1)S(1)}, bf16[48,768]{1,0:T(8,128)(2,1)S(1)}, u32[]{:S(2)}, u32[]{:S(2)}) collective-permute-start(bf16[48,768]{1,0:T(8,128)(2,1)S(1)} %add_convert_fusion.21), channel_id=1, source_target_pairs={{0,8},{8,16},{16,24},{24,28},{28,20},{20,12},{12,4},{4,0},{1,9},{9... | collective-permute-start | bytes 221192 | tf_op jit(solution)/shard_map/ppermute | solution.py:71
  485.0 8.7 %collective-permute-start.52 = (bf16[48,768]{1,0:T(8,128)(2,1)S(1)}, bf16[48,768]{1,0:T(8,128)(2,1)S(1)}, u32[]{:S(2)}, u32[]{:S(2)}) collective-permute-start(bf16[48,768]{1,0:T(8,128)(2,1)S(1)} %get-tuple-element.363), channel_id=1, source_target_pairs={{0,4},{8,0},{16,8},{24,16},{28,24},{20,28},{12,20},{4,12},{1,5},{9... | collective-permute-start | bytes 221192 | tf_op jit(solution)/shard_map/ppermute | solution.py:71
  493.3 41.7 %collective-permute-start.30 = (f32[16,32,768]{2,1,0:T(8,128)}, f32[16,32,768]{2,1,0:T(8,128)S(1)}, u32[]{:S(2)}, u32[]{:S(2)}) collective-permute-start(f32[16,32,768]{2,1,0:T(8,128)} %get-tuple-element.112), channel_id=1, source_target_pairs={{0,1},{1,0},{2,3},{3,2},{4,5},{5,4},{6,7},{7,6},{8,9},{9,8},{10,11... | collective-permute-start | bytes 4718600 | tf_op jit(solution)/shard_map/ppermute | solution.py:17
  498.2 17.8 %collective-permute-start.51 = (bf16[48,768]{1,0:T(8,128)(2,1)S(1)}, bf16[48,768]{1,0:T(8,128)(2,1)S(1)}, u32[]{:S(2)}, u32[]{:S(2)}) collective-permute-start(bf16[48,768]{1,0:T(8,128)(2,1)S(1)} %get-tuple-element.360), channel_id=1, source_target_pairs={{0,8},{8,16},{16,24},{24,28},{28,20},{20,12},{12,4},{4,0},{1,9},{9... | collective-permute-start | bytes 221192 | tf_op jit(solution)/shard_map/ppermute | solution.py:71
  500.5 8.6 %collective-permute-start.53 = (bf16[48,768]{1,0:T(8,128)(2,1)S(1)}, bf16[48,768]{1,0:T(8,128)(2,1)S(1)}, u32[]{:S(2)}, u32[]{:S(2)}) collective-permute-start(bf16[48,768]{1,0:T(8,128)(2,1)S(1)} %get-tuple-element.361), channel_id=1, source_target_pairs={{0,4},{8,0},{16,8},{24,16},{28,24},{20,28},{12,20},{4,12},{1,5},{9... | collective-permute-start | bytes 221192 | tf_op jit(solution)/shard_map/ppermute | solution.py:71
  512.1 11.5 %collective-permute-start.57 = (bf16[88,768]{1,0:T(8,128)(2,1)S(1)}, bf16[88,768]{1,0:T(8,128)(2,1)S(1)}, u32[]{:S(2)}, u32[]{:S(2)}) collective-permute-start(bf16[88,768]{1,0:T(8,128)(2,1)S(1)} %add_convert_fusion.16), channel_id=1, source_target_pairs={{0,8},{8,16},{16,24},{24,28},{28,20},{20,12},{12,4},{4,0},{1,9},{9... | collective-permute-start | bytes 405512 | tf_op jit(solution)/shard_map/ppermute | solution.py:71
  523.7 8.3 %collective-permute-start.58 = (bf16[88,768]{1,0:T(8,128)(2,1)S(1)}, bf16[88,768]{1,0:T(8,128)(2,1)S(1)}, u32[]{:S(2)}, u32[]{:S(2)}) collective-permute-start(bf16[88,768]{1,0:T(8,128)(2,1)S(1)} %add_convert_fusion.15), channel_id=1, source_target_pairs={{0,8},{8,16},{16,24},{24,28},{28,20},{20,12},{12,4},{4,0},{1,9},{9... | collective-permute-start | bytes 405512 | tf_op jit(solution)/shard_map/ppermute | solution.py:71
  532.7 49.1 %collective-permute-start.59 = (bf16[88,768]{1,0:T(8,128)(2,1)}, bf16[88,768]{1,0:T(8,128)(2,1)}, u32[]{:S(2)}, u32[]{:S(2)}) collective-permute-start(bf16[88,768]{1,0:T(8,128)(2,1)} %get-tuple-element.349), channel_id=1, source_target_pairs={{0,8},{8,16},{16,24},{24,28},{28,20},{20,12},{12,4},{4,0},{1,9},{9... | collective-permute-start | bytes 405512 | tf_op jit(solution)/shard_map/ppermute | solution.py:71
  532.8 46.9 %collective-permute-start.61 = (bf16[88,768]{1,0:T(8,128)(2,1)}, bf16[88,768]{1,0:T(8,128)(2,1)}, u32[]{:S(2)}, u32[]{:S(2)}) collective-permute-start(bf16[88,768]{1,0:T(8,128)(2,1)} %get-tuple-element.350), channel_id=1, source_target_pairs={{0,4},{8,0},{16,8},{24,16},{28,24},{20,28},{12,20},{4,12},{1,5},{9... | collective-permute-start | bytes 405512 | tf_op jit(solution)/shard_map/ppermute | solution.py:71
  566.4 25.8 %collective-permute-start.31 = (bf16[16,32,384]{2,1,0:T(8,128)(2,1)}, bf16[16,32,384]{2,1,0:T(8,128)(2,1)}, u32[]{:S(2)}, u32[]{:S(2)}) collective-permute-start(bf16[16,32,384]{2,1,0:T(8,128)(2,1)} %select_convert_fusion.1), channel_id=1, source_target_pairs={{0,2},{2,0},{1,3},{3,1},{4,6},{6,4},{5,7},{7,5},{8,10},{10,8},{9,1... | collective-permute-start | bytes 1179656 | tf_op jit(solution)/shard_map/ppermute | solution.py:17
  577.7 9.6 %collective-permute-start.32 = (bf16[16,32,384]{2,1,0:T(8,128)(2,1)}, bf16[16,32,384]{2,1,0:T(8,128)(2,1)}, u32[]{:S(2)}, u32[]{:S(2)}) collective-permute-start(bf16[16,32,384]{2,1,0:T(8,128)(2,1)} %select_convert_fusion), channel_id=1, source_target_pairs={{0,2},{2,0},{1,3},{3,1},{4,6},{6,4},{5,7},{7,5},{8,10},{10,8},{9,1... | collective-permute-start | bytes 1179656 | tf_op jit(solution)/shard_map/ppermute | solution.py:17
  592.2 15.6 %collective-permute-start.42 = (f32[166,128]{1,0:T(8,128)S(1)}, f32[166,128]{1,0:T(8,128)}, u32[]{:S(2)}, u32[]{:S(2)}) collective-permute-start(f32[166,128]{1,0:T(8,128)S(1)} %bitcast.346), channel_id=1, source_target_pairs={{0,1},{1,0},{2,3},{3,2},{4,5},{5,4},{6,7},{7,6},{8,9},{9,8},{10,11... | collective-permute-start | bytes 254984 | tf_op jit(solution)/shard_map/ppermute | solution.py:17
  605.6 40.7 %collective-permute-start.34 = (bf16[8,48,1536]{2,1,0:T(8,128)(2,1)S(1)}, bf16[8,48,1536]{2,1,0:T(8,128)(2,1)S(1)}, u32[]{:S(2)}, u32[]{:S(2)}) collective-permute-start(bf16[8,48,1536]{2,1,0:T(8,128)(2,1)S(1)} %fusion.64), channel_id=1, source_target_pairs={{0,2},{2,0},{1,3},{3,1},{4,6},{6,4},{5,7},{7,5},{8,10},{10,8},{9,1... | collective-permute-start | bytes 3538952 | tf_op jit(solution)/shard_map/ppermute | solution.py:17
  608.7 27.5 %collective-permute-start.43 = (f32[166,128]{1,0:T(8,128)S(1)}, f32[166,128]{1,0:T(8,128)S(1)}, u32[]{:S(2)}, u32[]{:S(2)}) collective-permute-start(f32[166,128]{1,0:T(8,128)S(1)} %bitcast_add_fusion.3), channel_id=1, source_target_pairs={{0,2},{2,0},{1,3},{3,1},{4,6},{6,4},{5,7},{7,5},{8,10},{10,8},{9,1... | collective-permute-start | bytes 254984 | tf_op jit(solution)/shard_map/ppermute | solution.py:17
  648.1 30.2 %collective-permute-start.33 = (f32[16,32,768]{2,1,0:T(8,128)S(1)}, f32[16,32,768]{2,1,0:T(8,128)}, u32[]{:S(2)}, u32[]{:S(2)}) collective-permute-start(f32[16,32,768]{2,1,0:T(8,128)S(1)} %add_add_fusion.3), channel_id=1, source_target_pairs={{0,1},{1,0},{2,3},{3,2},{4,5},{5,4},{6,7},{7,6},{8,9},{9,8},{10,11... | collective-permute-start | bytes 4718600 | tf_op jit(solution)/shard_map/ppermute | solution.py:17
  656.9 10.5 %collective-permute-start.39 = (bf16[48,1536]{1,0:T(8,128)(2,1)S(1)}, bf16[48,1536]{1,0:T(8,128)(2,1)S(1)}, u32[]{:S(2)}, u32[]{:S(2)}) collective-permute-start(bf16[48,1536]{1,0:T(8,128)(2,1)S(1)} %get-tuple-element.348), channel_id=1, source_target_pairs={{0,4},{8,0},{16,8},{24,16},{28,24},{20,28},{12,20},{4,12},{1,5},{9... | collective-permute-start | bytes 442376 | tf_op jit(solution)/shard_map/ppermute | solution.py:71
  671.5 9.8 %collective-permute-start.38 = (bf16[48,1536]{1,0:T(8,128)(2,1)S(1)}, bf16[48,1536]{1,0:T(8,128)(2,1)S(1)}, u32[]{:S(2)}, u32[]{:S(2)}) collective-permute-start(bf16[48,1536]{1,0:T(8,128)(2,1)S(1)} %get-tuple-element.345), channel_id=1, source_target_pairs={{0,8},{8,16},{16,24},{24,28},{28,20},{20,12},{12,4},{4,0},{1,9},{9... | collective-permute-start | bytes 442376 | tf_op jit(solution)/shard_map/ppermute | solution.py:71
  (137 other events, 2002.3 us)
Sparse Core Ops, SparseCore 0:
  17.2 106.4 all-gather.1
  460.7 108.8 reduce-scatter.1

commit v2 on v1

v2 whole, which is shorter than its diff:
```python
import math

import jax
import jax.numpy as jnp
from jax import lax
from jax.experimental import pallas as pl
from jax.experimental.pallas import tpu as pltpu
from jax.sharding import PartitionSpec as P

HEAD_DIM = 64
EPS = 1e-06
NEG = -1e30
BF = jnp.bfloat16
F32 = jnp.float32


def partner(shard, axis, distance):
    return lax.ppermute(shard, axis, [(i, i ^ 1 << distance) for i in range(lax.axis_size(axis))])


def ring_of(count):
    return list(range(0, count, 2)) + list(range(1, count, 2))[::-1]


def ring_place(count):
    order = ring_of(count)
    places = [order.index(i) for i in range(count)]
    return order, jnp.asarray(places, jnp.int32)[lax.axis_index("items")]


def shift_ring(shard, order, step):
    count = len(order)
    return lax.ppermute(
        shard, "items", [(order[i], order[(i + step) % count]) for i in range(count)]
    )


def gather_items(shard):
    count = lax.axis_size("items")
    order, place = ring_place(count)
    table = jnp.asarray(order, jnp.int32)
    rows = shard.shape[0]
    whole = jnp.zeros((count * rows,) + shard.shape[1:], shard.dtype)

    def put(whole, piece, distance):
        start = table[(place + distance) % count] * rows
        return lax.dynamic_update_slice_in_dim(whole, piece, start, 0)

    whole = put(whole, shard, 0)
    up = down = shard
    for hop in range(1, count // 2 + 1):
        up = shift_ring(up, order, 1)
        whole = put(whole, up, count - hop)
        if hop <= (count - 1) // 2:
            down = shift_ring(down, order, -1)
            whole = put(whole, down, hop)
    return whole


def pair_streams(shard):
    other = partner(shard, "stream", 0)
    first = lax.axis_index("stream") == 0
    return jnp.where(
        first, jnp.concatenate([shard, other], axis=0), jnp.concatenate([other, shard], axis=0)
    )


def scatter_items(total):
    count = lax.axis_size("items")
    order, place = ring_place(count)
    table = jnp.asarray(order, jnp.int32)
    rows = total.shape[0] // count

    def piece(distance):
        start = table[(place + distance) % count] * rows
        return lax.dynamic_slice_in_dim(total, start, rows, 0).astype(F32)

    far_up, far_down = count // 2, (count - 1) // 2
    result = piece(0)
    up = down = None
    for hop in range(far_up, 0, -1):
        own = piece(hop)
        up = shift_ring((own if up is None else own + up).astype(BF), order, 1).astype(F32)
        if hop <= far_down:
            own = piece(count - hop)
            down = shift_ring((own if down is None else own + down).astype(BF), order, -1).astype(F32)
    return result + up + down


def scatter_both(total):
    count = lax.axis_size("items")
    rows = total.shape[0] // (2 * count)
    parts = total.reshape((count, 2, rows, total.shape[1]))
    stream = lax.axis_index("stream")
    keep = lax.dynamic_index_in_dim(parts, stream, 1, keepdims=False)
    away = lax.dynamic_index_in_dim(parts, 1 - stream, 1, keepdims=False)
    arrived = partner(away, "stream", 0)
    both = keep.astype(F32) + arrived.astype(F32)
    return scatter_items(both.reshape(count * rows, total.shape[1]))


def all_total(vector):
    vector = vector + partner(vector, "heads", 0)
    vector = vector + partner(vector, "stream", 0)
    bit = 0
    while (1 << bit) < lax.axis_size("items"):
        vector = vector + partner(vector, "items", bit)
        bit += 1
    return vector


def all_totals(arrays):
    sizes = [math.prod(one.shape) for one in arrays]
    packed = jnp.concatenate([one.reshape(-1) for one in arrays]).reshape(-1, 128)
    total = all_total(packed).reshape(-1)
    results, start = [], 0
    for one, size in zip(arrays, sizes):
        results.append(total[start : start + size].reshape(one.shape))
        start += size
    return tuple(results)


def spread(piece, start, full_len):
    return lax.dynamic_update_slice_in_dim(jnp.zeros((full_len,), F32), piece, start, 0)


def mul(left, right):
    return jnp.dot(left, right, preferred_element_type=F32)


def mul_t(left, right):
    return lax.dot_general(left, right, (((1,), (1,)), ((), ())), preferred_element_type=F32)


def t_mul(left, right):
    return lax.dot_general(left, right, (((0,), (0,)), ((), ())), preferred_element_type=F32)


def standard(rows):
    center = rows - jnp.mean(rows, axis=-1, keepdims=True)
    scale = lax.rsqrt(jnp.mean(center * center, axis=-1, keepdims=True) + EPS)
    return center * scale, scale


def norm_back(grad, unit, scale, gain):
    inner = grad * gain
    return scale * (
        inner
        - jnp.mean(inner, axis=-1, keepdims=True)
        - unit * jnp.mean(inner * unit, axis=-1, keepdims=True)
    )


def total_rows(rows):
    return jnp.sum(rows, axis=0, keepdims=True)


def head_mask(rows, heads, value, dtype):
    row = lax.broadcasted_iota(jnp.int32, (heads * rows, heads * HEAD_DIM), 0) // rows
    col = lax.broadcasted_iota(jnp.int32, (heads * rows, heads * HEAD_DIM), 1) // HEAD_DIM
    return jnp.where(row == col, value, 0.0).astype(dtype)


def stack_heads(rows, heads, mask):
    return jnp.concatenate([rows] * heads, axis=0) * mask


def fold_heads(stacked, heads, mask):
    rows = stacked.shape[0] // heads
    stacked = stacked * mask
    result = stacked[:rows]
    for head in range(1, heads):
        result = result + stacked[head * rows : (head + 1) * rows]
    return result


def softmax(scores):
    power = jnp.exp(scores - jnp.max(scores, axis=-1, keepdims=True))
    return power * (1.0 / jnp.sum(power, axis=-1, keepdims=True))


def attend(queries, keys, values, hide, heads, scaled_mask, out_mask):
    scores = hide(mul_t(stack_heads(queries, heads, scaled_mask), keys))
    weights = softmax(scores).astype(BF)
    return fold_heads(mul(weights, values), heads, out_mask).astype(BF)


def attend_back(queries, keys, values, grad, hide, heads, scaled_mask, plain_mask, out_mask):
    queries = stack_heads(queries, heads, scaled_mask)
    grad = stack_heads(grad, heads, plain_mask)
    weights = softmax(hide(mul_t(queries, keys)))
    grad_weights = mul_t(grad, values)
    grad_values = t_mul(weights.astype(BF), grad)
    delta = jnp.sum(grad_weights * weights, axis=-1, keepdims=True)
    grad_scores = (weights * (grad_weights - delta)).astype(BF)
    grad_queries = fold_heads(mul(grad_scores, keys), heads, out_mask) * HEAD_DIM ** (-0.5)
    return grad_queries, t_mul(grad_scores, queries), grad_values


def whole(shape):
    return pl.BlockSpec(shape, lambda i: (0,) * len(shape))


def block(shape):
    return pl.BlockSpec(shape, lambda i: (i,) + (0,) * (len(shape) - 1))


def column(shape):
    return pl.BlockSpec(shape, lambda i: (0, i))


def shaped(shape, dtype):
    return jax.ShapeDtypeStruct(shape, dtype)


def call(kernel, grid, in_specs, out_specs, out_shape, scratch=(), flops=0, moved=0):
    return pl.pallas_call(
        kernel,
        grid=(grid,),
        in_specs=in_specs,
        out_specs=out_specs,
        out_shape=out_shape,
        scratch_shapes=list(scratch),
        compiler_params=pltpu.CompilerParams(
            dimension_semantics=("arbitrary",), vmem_limit_bytes=56 << 20
        ),
        cost_estimate=pl.CostEstimate(flops=flops, bytes_accessed=moved, transcendentals=0),
    )


def feature_norm(features, gain, shift, padded):
    items, patches, width = features.shape

    def kernel(feat, gain, shift, out):
        unit, _ = standard(feat[0].astype(F32))
        out[0, :patches] = (unit * gain[...] + shift[...]).astype(BF)
        out[0, patches:] = jnp.zeros((padded - patches, width), BF)

    return call(
        kernel,
        items,
        [block((1, patches, width)), whole((1, width)), whole((1, width))],
        block((1, padded, width)),
        shaped((items, padded, width), BF),
        moved=4 * items * patches * width,
    )(features, gain, shift)


def project(own, far, weight, bias):
    rows, width = own.shape
    cols = weight.shape[1]
    head_cols = cols // 3
    step = rows // 4

    def kernel(own, far, weight, bias, q, kv, kv_far):
        near = mul(own[...], weight[...]) + bias[...]
        q[...] = near[:, :head_cols].astype(BF)
        kv[...] = near[:, head_cols:].astype(BF)
        kv_far[...] = (mul(far[...], weight[:, head_cols:]) + bias[:, head_cols:]).astype(BF)

    return call(
        kernel,
        4,
        [block((step, width)), block((step, width)), whole((width, cols)), whole((1, cols))],
        [block((step, head_cols)), block((step, 2 * head_cols)), block((step, 2 * head_cols))],
        [shaped((rows, head_cols), BF)] + [shaped((rows, 2 * head_cols), BF)] * 2,
        flops=10 * rows * width * head_cols,
        moved=4 * rows * width + 2 * width * cols,
    )(own, far, weight, bias)


def self_attention(q, kv, kv_far, allowed, weight, items, batch):
    rows, cols = q.shape
    heads, each = cols // HEAD_DIM, rows // items
    width = weight.shape[0]

    def kernel(q, kv, kv_far, allowed, weight, attended, out):
        index = pl.program_id(0)
        scaled = head_mask(each, heads, HEAD_DIM ** (-0.5), BF)
        ones = head_mask(each, heads, 1.0, F32)
        for item in range(batch):
            span = slice(item * each, (item + 1) * each)
            keys = jnp.concatenate([kv[span, :cols], kv_far[span, :cols]], axis=0)
            values = jnp.concatenate([kv[span, cols:], kv_far[span, cols:]], axis=0)
            seen = jnp.concatenate([allowed[item]] * heads, axis=0) > 0
            result = attend(
                q[span], keys, values, lambda s: jnp.where(seen, s, NEG), heads, scaled, ones
            )
            start = pl.multiple_of((index * batch + item) * each, each)
            attended[pl.ds(start, each), :] = result

        @pl.when(index == pl.num_programs(0) - 1)
        def _():
            out[...] = mul_t(attended[...], weight[...])

    part = batch * each
    return call(
        kernel,
        items // batch,
        [
            block((part, cols)),
            block((part, 2 * cols)),
            block((part, 2 * cols)),
            block((batch, each, 2 * each)),
            whole((width, cols)),
        ],
        [whole((rows, cols)), whole((rows, width))],
        [shaped((rows, cols), BF), shaped((rows, width), F32)],
        flops=2 * rows * cols * width * 3,
        moved=rows * cols * 14 + rows * width * 4,
    )(q, kv, kv_far, allowed, weight)


def cross_attention(own, near, away, rows_in, cq, keys_values, weight, items, batch, patches):
    rows, width = own.shape
    cols = weight.shape[1]
    heads, each = cols // HEAD_DIM, rows // items
    padded = keys_values.shape[1]

    def kernel(own, near, away, bias, gain, shift, bias_q, cq, kv, weight, unit, scale, low, qc, attended, out):
        index = pl.program_id(0)

        @pl.when(index == 0)
        def _():
            one, size = standard(own[...].astype(F32) + near[...] + away[...] + bias[...])
            unit[...] = one
            scale[...] = size
            low[...] = (one * gain[...] + shift[...]).astype(BF)
            qc[...] = (mul(low[...], cq[...]) + bias_q[...]).astype(BF)

        scaled = head_mask(each, heads, HEAD_DIM ** (-0.5), BF)
        ones = head_mask(each, heads, 1.0, F32)
        real = lax.broadcasted_iota(jnp.int32, (heads * each, padded), 1) < patches
        for item in range(batch):
            start = pl.multiple_of((index * batch + item) * each, each)
            attended[pl.ds(start, each), :] = attend(
                qc[pl.ds(start, each), :],
                kv[item, :, :cols],
                kv[item, :, cols:],
                lambda s: jnp.where(real, s, NEG),
                heads,
                scaled,
                ones,
            )

        @pl.when(index == pl.num_programs(0) - 1)
        def _():
            out[...] = mul_t(attended[...], weight[...])

    bias, gain, shift, bias_q = rows_in
    return call(
        kernel,
        items // batch,
        [whole((rows, width))] * 3
        + [whole((1, width))] * 3
        + [whole((1, cols)), whole((width, cols)), block((batch, padded, 2 * cols)), whole((width, cols))],
        [
            whole((rows, width)),
            whole((rows, 1)),
            whole((rows, width)),
            whole((rows, cols)),
            whole((rows, cols)),
            whole((rows, width)),
        ],
        [
            shaped((rows, width), F32),
            shaped((rows, 1), F32),
            shaped((rows, width), BF),
            shaped((rows, cols), BF),
            shaped((rows, cols), BF),
            shaped((rows, width), F32),
        ],
        flops=2 * rows * cols * padded * heads * 2,
        moved=rows * width * 20 + 4 * items * padded * cols,
    )(own, near, away, bias, gain, shift, bias_q, cq, keys_values, weight)


def feed_forward(flag, unit, near, away, rows_in, w_in, b_in, w_out, chunk):
    rows, width = unit.shape
    hidden = w_in.shape[1]

    def kernel(flag, unit, near, away, gain0, shift0, bias, gain1, shift1, w_in, b_in, w_out, z, z_low, unit2, scale2, act, slope, out):
        @pl.when(pl.program_id(0) == 0)
        def _():
            after = unit[...] * gain0[...] + shift0[...]
            one, size = standard(after + near[...] + away[...] + bias[...])
            unit2[...] = one
            scale2[...] = size
            z[...] = jnp.where(flag[0] == 0, one * gain1[...] + shift1[...], after)
            z_low[...] = z[...].astype(BF)
            out[...] = jnp.zeros_like(out)

        for half in range(2):
            span = slice(half * rows // 2, (half + 1) * rows // 2)
            u = mul(z_low[span], w_in[...]) + b_in[...]
            share = 0.5 + 0.5 * lax.erf(u * math.sqrt(0.5))
            act_half = (u * share).astype(BF)
            act[span] = act_half
            slope[span] = share + u * (jnp.exp(-0.5 * u * u) * (1.0 / math.sqrt(2.0 * math.pi)))
            out[span] += mul_t(act_half, w_out[...])

    row = whole((1, width))
    return call(
        kernel,
        hidden // chunk,
        [pl.BlockSpec(memory_space=pltpu.SMEM)]
        + [whole((rows, width))] * 3
        + [row] * 5
        + [column((width, chunk)), column((1, chunk)), column((width, chunk))],
        [
            whole((rows, width)),
            whole((rows, width)),
            whole((rows, width)),
            whole((rows, 1)),
            column((rows, chunk)),
            column((rows, chunk)),
            whole((rows, width)),
        ],
        [
            shaped((rows, width), F32),
            shaped((rows, width), BF),
            shaped((rows, width), F32),
            shaped((rows, 1), F32),
            shaped((rows, hidden), BF),
            shaped((rows, hidden), F32),
            shaped((rows, width), F32),
        ],
        flops=4 * rows * hidden * width,
        moved=rows * width * 26 + rows * hidden * 6 + width * hidden * 4,
    )(flag, unit, near, away, *rows_in, w_in, b_in, w_out)


def feed_back(z, near, away, cotangent, rows_in, slope, w_in, w_out, chunk):
    rows, width = z.shape
    hidden = w_in.shape[1]

    def kernel(z, near, away, cot, bias, gain, shift, slope, w_in, w_out, result, grad_v, grad_u, grad_pre, out, sums, sum_pre):
        @pl.when(pl.program_id(0) == 0)
        def _():
            one, size = standard(z[...] + near[...] + away[...] + bias[...])
            dy = cot[...]
            result[...] = (one * gain[...] + shift[...]).astype(BF)
            grad_v[...] = norm_back(dy, one, size, gain[...])
            grad_u[...] = grad_v[...].astype(BF)
            sums[0:1] = total_rows(dy * one)
            sums[1:2] = total_rows(dy)
            sums[2:3] = total_rows(grad_u[...].astype(F32))
            out[...] = jnp.zeros_like(out)

        for half in range(2):
            span = slice(half * rows // 2, (half + 1) * rows // 2)
            pre = (mul(grad_u[span], w_out[...]) * slope[span]).astype(BF)
            grad_pre[span] = pre
            out[span] += mul_t(pre, w_in[...])
        sum_pre[...] = total_rows(grad_pre[...].astype(F32))

    row = whole((1, width))
    return call(
        kernel,
        hidden // chunk,
        [whole((rows, width))] * 4
        + [row] * 3
        + [column((rows, chunk)), column((width, chunk)), column((width, chunk))],
        [
            whole((rows, width)),
            whole((rows, width)),
            whole((rows, width)),
            column((rows, chunk)),
            whole((rows, width)),
            whole((8, width)),
            column((1, chunk)),
        ],
        [
            shaped((rows, width), BF),
            shaped((rows, width), F32),
            shaped((rows, width), BF),
            shaped((rows, hidden), BF),
            shaped((rows, width), F32),
            shaped((8, width), F32),
            shaped((1, hidden), F32),
        ],
        flops=4 * rows * hidden * width,
        moved=rows * width * 28 + rows * hidden * 6 + width * hidden * 4,
    )(z, near, away, cotangent, *rows_in, slope, w_in, w_out)


def cross_back(flag, grad_v, near, away, unit2, scale2, gain, qc, keys_values, weight, cq, items, batch, patches):
    rows, width = grad_v.shape
    cols = weight.shape[1]
    heads, each = cols // HEAD_DIM, rows // items
    padded = keys_values.shape[1]

    def kernel(flag, grad_v, near, away, unit2, scale2, gain, qc, kv, weight, cq, after, mix, grad_qc, grad_kv, out, sums, sums_c, grad_att):
        index = pl.program_id(0)

        @pl.when(index == 0)
        def _():
            dz = grad_v[...] + near[...] + away[...]
            mine = flag[0] == 0
            used = jnp.where(mine, dz, 0.0)
            two = norm_back(used, unit2[...], scale2[...], gain[...])
            after[...] = jnp.where(mine, two, dz)
            mix[...] = two.astype(BF)
            grad_att[...] = mul(mix[...], weight[...]).astype(BF)
            sums[0:1] = total_rows(used * unit2[...])
            sums[1:2] = total_rows(used)
            sums[2:3] = total_rows(mix[...].astype(F32))
            sums_c[...] = jnp.zeros_like(sums_c)

        root = HEAD_DIM ** (-0.5)
        scaled = head_mask(each, heads, root, BF)
        plain = head_mask(each, heads, 1.0, BF)
        ones = head_mask(each, heads, 1.0, F32)
        real = lax.broadcasted_iota(jnp.int32, (heads * each, padded), 1) < patches
        for item in range(batch):
            start = pl.multiple_of((index * batch + item) * each, each)
            dq, dk, dv = attend_back(
                qc[pl.ds(start, each), :],
                kv[item, :, :cols],
                kv[item, :, cols:],
                grad_att[pl.ds(start, each), :],
                lambda s: jnp.where(real, s, NEG),
                heads,
                scaled,
                plain,
                ones,
            )
            grad_qc[pl.ds(start, each), :] = dq.astype(BF)
            dk, dv = dk.astype(BF), dv.astype(BF)
            grad_kv[item, :, :cols] = dk
            grad_kv[item, :, cols:] = dv
            sums_c[1:2] += total_rows(dk.astype(F32))
            sums_c[2:3] += total_rows(dv.astype(F32))

        @pl.when(index == pl.num_programs(0) - 1)
        def _():
            out[...] = mul_t(grad_qc[...], cq[...])
            sums_c[0:1] = total_rows(grad_qc[...].astype(F32))

    return call(
        kernel,
        items // batch,
        [pl.BlockSpec(memory_space=pltpu.SMEM)]
        + [whole((rows, width))] * 4
        + [
            whole((rows, 1)),
            whole((1, width)),
            whole((rows, cols)),
            block((batch, padded, 2 * cols)),
            whole((width, cols)),
            whole((width, cols)),
        ],
        [
            whole((rows, width)),
            whole((rows, width)),
            whole((rows, cols)),
            block((batch, padded, 2 * cols)),
            whole((rows, width)),
            whole((8, width)),
            whole((8, cols)),
        ],
        [
            shaped((rows, width), F32),
            shaped((rows, width), BF),
            shaped((rows, cols), BF),
            shaped((items, padded, 2 * cols), BF),
            shaped((rows, width), F32),
            shaped((8, width), F32),
            shaped((8, cols), F32),
        ],
        scratch=[pltpu.VMEM((rows, cols), BF)],
        flops=2 * rows * cols * padded * heads * 5,
        moved=rows * width * 26 + 8 * items * padded * cols,
    )(flag, grad_v, near, away, unit2, scale2, gain, qc, keys_values, weight, cq)


def self_back(after, near, away, unit, scale, gain, q, kv, kv_far, allowed, weight, w_qkv, items, batch):
    rows, width = after.shape
    cols = weight.shape[1]
    heads, each = cols // HEAD_DIM, rows // items

    def kernel(after, near, away, unit, scale, gain, q, kv, kv_far, allowed, weight, w_qkv, grad_one, mix, grad_near, grad_away, out, out_far, sums, sums_c, grad_att):
        index = pl.program_id(0)

        @pl.when(index == 0)
        def _():
            grad = after[...] + near[...] + away[...]
            grad_one[...] = norm_back(grad, unit[...], scale[...], gain[...])
            mix[...] = grad_one[...].astype(BF)
            grad_att[...] = mul(mix[...], weight[...]).astype(BF)
            sums[0:1] = total_rows(grad * unit[...])
            sums[1:2] = total_rows(grad)
            sums[2:3] = total_rows(mix[...].astype(F32))

        scaled = head_mask(each, heads, HEAD_DIM ** (-0.5), BF)
        plain = head_mask(each, heads, 1.0, BF)
        ones = head_mask(each, heads, 1.0, F32)
        for item in range(batch):
            span = slice(item * each, (item + 1) * each)
            start = pl.multiple_of((index * batch + item) * each, each)
            keys = jnp.concatenate([kv[span, :cols], kv_far[span, :cols]], axis=0)
            values = jnp.concatenate([kv[span, cols:], kv_far[span, cols:]], axis=0)
            seen = jnp.concatenate([allowed[item]] * heads, axis=0) > 0
            dq, dk, dv = attend_back(
                q[span],
                keys,
                values,
                grad_att[pl.ds(start, each), :],
                lambda s: jnp.where(seen, s, NEG),
                heads,
                scaled,
                plain,
                ones,
            )
            grad_near[pl.ds(start, each), :cols] = dq.astype(BF)
            grad_near[pl.ds(start, each), cols : 2 * cols] = dk[:each].astype(BF)
            grad_near[pl.ds(start, each), 2 * cols :] = dv[:each].astype(BF)
            grad_away[pl.ds(start, each), :cols] = dk[each:].astype(BF)
            grad_away[pl.ds(start, each), cols:] = dv[each:].astype(BF)

        @pl.when(index == pl.num_programs(0) - 1)
        def _():
            out[...] = mul_t(grad_near[...], w_qkv[...])
            out_far[...] = mul_t(grad_away[...], w_qkv[:, cols:])
            sums_c[0:1] = total_rows(grad_near[...].astype(F32))
            sums_c[1:2, cols:] = total_rows(grad_away[...].astype(F32))

    part = batch * each
    return call(
        kernel,
        items // batch,
        [whole((rows, width))] * 4
        + [
            whole((rows, 1)),
            whole((1, width)),
            block((part, cols)),
            block((part, 2 * cols)),
            block((part, 2 * cols)),
            block((batch, each, 2 * each)),
            whole((width, cols)),
            whole((width, 3 * cols)),
        ],
        [
            whole((rows, width)),
            whole((rows, width)),
            whole((rows, 3 * cols)),
            whole((rows, 2 * cols)),
            whole((rows, width)),
            whole((rows, width)),
            whole((8, width)),
            whole((8, 3 * cols)),
        ],
        [
            shaped((rows, width), F32),
            shaped((rows, width), BF),
            shaped((rows, 3 * cols), BF),
            shaped((rows, 2 * cols), BF),
            shaped((rows, width), F32),
            shaped((rows, width), F32),
            shaped((8, width), F32),
            shaped((8, 3 * cols), F32),
        ],
        scratch=[pltpu.VMEM((rows, cols), BF)],
        flops=2 * rows * cols * width * 9,
        moved=rows * width * 32 + rows * cols * 20,
    )(after, near, away, unit, scale, gain, q, kv, kv_far, allowed, weight, w_qkv)


def visible(stream, segments, modes):
    same_caption = segments[:, :, None] == segments[:, None, :]
    own = jnp.logical_or(stream == 0, same_caption)
    far = jnp.where(stream == 0, modes == 2, modes >= 1)[:, None, None]
    return jnp.concatenate([own, jnp.broadcast_to(far, own.shape)], axis=2).astype(F32)


def body(
    hidden,
    features,
    segments,
    modes,
    w_qkv,
    self_bias,
    self_out,
    cross_q,
    cross_kv,
    cross_bias,
    cross_out,
    gains,
    shifts,
    feat_gain,
    feat_shift,
    ffn_in,
    ffn_bias_in,
    ffn_out,
    ffn_bias_out,
    cotangent,
):
    stream = lax.axis_index("stream")
    head_index = lax.axis_index("heads")
    query_mask = (stream == 0).astype(F32)
    text_mask = 1.0 - query_mask
    lead_mask = (head_index == 0).astype(F32)
    items, _, each, width = hidden.shape
    rows = items * each
    half = rows // 2
    cols = w_qkv.shape[2]
    hidden_cols = ffn_in.shape[2]
    patches, feat_width = features.shape[1:]
    padded = (patches + 7) // 8 * 8
    col_start = head_index * cols
    hidden_start = head_index * hidden_cols
    flag = stream.astype(jnp.int32).reshape(1)

    three = [slice(i * cols, (i + 1) * cols) for i in range(3)]
    qkv_all = gather_items(pair_streams(jnp.concatenate([w_qkv[0], w_qkv[1], w_qkv[2]], axis=1)))
    own = hidden.reshape(rows, width)
    my_half = lax.dynamic_slice_in_dim(own, head_index * half, half, 0)
    far_half = partner(my_half, "stream", 0)
    far_other = partner(far_half, "heads", 0)
    far = jnp.where(
        head_index == 0,
        jnp.concatenate([far_half, far_other], axis=0),
        jnp.concatenate([far_other, far_half], axis=0),
    )
    kv_all = gather_items(pair_streams(jnp.concatenate([cross_kv[0], cross_kv[1]], axis=1)))
    rest_all = gather_items(
        pair_streams(jnp.concatenate([self_out.T, cross_q, cross_out.T], axis=1))
    )
    self_out_t, cross_q_all, cross_out_t = (rest_all[:, one] for one in three)
    ffn_all = lax.all_gather(
        jnp.concatenate([ffn_in[0], ffn_out[0].T], axis=1), "items", axis=0, tiled=True
    )
    inner, outer_t = ffn_all[:, :hidden_cols], ffn_all[:, hidden_cols:]

    def my_cols(vector):
        return lax.dynamic_slice_in_dim(vector, col_start, cols, 0)

    def row(vector):
        return vector.reshape(1, -1)

    none = jnp.zeros((cols,), F32)
    bias_qkv = row(jnp.concatenate([my_cols(self_bias[0]), none, my_cols(self_bias[1])]))
    bias_kv = row(jnp.concatenate([none, my_cols(cross_bias[1])]))
    gain_ffn = row(lax.dynamic_index_in_dim(gains, 2 + stream, 0, keepdims=False))
    shift_ffn = row(lax.dynamic_index_in_dim(shifts, 2 + stream, 0, keepdims=False))
    bias_in = row(
        lax.dynamic_slice_in_dim(
            lax.dynamic_index_in_dim(ffn_bias_in, stream, 0, keepdims=False),
            hidden_start,
            hidden_cols,
            0,
        )
    )
    bias_out = row(lax.dynamic_index_in_dim(ffn_bias_out, stream, 0, keepdims=False))

    def swap(part):
        return partner(part, "heads", 0)

    feat_norm = feature_norm(features, row(feat_gain), row(feat_shift), padded)
    feat_rows = feat_norm.reshape(items * padded, feat_width)
    q, kv, kv_far = project(own, far, qkv_all, bias_qkv)
    allowed = visible(stream, segments, modes)
    attended, part = self_attention(q, kv, kv_far, allowed, self_out_t, items, 4)
    keys_values = (mul(feat_rows, kv_all) + bias_kv).astype(BF).reshape(items, padded, 2 * cols)
    unit_one, scale_one, after_low, qc, attended_c, part_c = cross_attention(
        own,
        part,
        swap(part),
        (row(self_bias[2]), row(gains[0]), row(shifts[0]), row(my_cols(cross_bias[0]))),
        cross_q_all,
        keys_values,
        cross_out_t,
        items,
        2,
        patches,
    )
    z, z_low, unit_two, scale_two, activated, slope, part_f = feed_forward(
        flag,
        unit_one,
        part_c,
        swap(part_c),
        (row(gains[0]), row(shifts[0]), row(cross_bias[2]), row(gains[1]), row(shifts[1])),
        inner,
        bias_in,
        outer_t,
        256,
    )

    output, grad_three, grad_u, grad_pre, part_z, sums_three, sum_pre = feed_back(
        z,
        part_f,
        swap(part_f),
        cotangent.reshape(rows, width),
        (bias_out, gain_ffn, shift_ffn),
        slope,
        inner,
        outer_t,
        256,
    )
    away_z = swap(part_z)
    ffn_grad = jnp.concatenate(
        [t_mul(z_low, grad_pre).astype(BF), t_mul(grad_u, activated).astype(BF)], axis=1
    )
    ffn_red = lax.psum_scatter(ffn_grad, "items", scatter_dimension=0, tiled=True).astype(F32)
    grad_after, mix_c, grad_qc, grad_kv, part_a, sums_two, sums_cross = cross_back(
        flag,
        grad_three,
        part_z,
        away_z,
        unit_two,
        scale_two,
        row(gains[1]),
        qc,
        keys_values,
        cross_out_t,
        cross_q_all,
        items,
        2,
        patches,
    )
    away_a = swap(part_a)
    cross_grad = jnp.concatenate(
        [t_mul(after_low, grad_qc).astype(BF), t_mul(mix_c, attended_c).astype(BF)], axis=1
    )
    kv_grad = t_mul(feat_rows, grad_kv.reshape(items * padded, 2 * cols))
    grad_one, mix, grad_near, grad_away, part_h, part_far, sums_one, sums_self = self_back(
        grad_after,
        part_a,
        away_a,
        unit_one,
        scale_one,
        row(gains[0]),
        q,
        kv,
        kv_far,
        allowed,
        self_out_t,
        qkv_all,
        items,
        4,
    )
    self_grad = jnp.concatenate(
        [
            t_mul(own, grad_near[:, :cols]).astype(BF),
            (t_mul(own, grad_near[:, cols:]) + t_mul(far, grad_away)).astype(BF),
            t_mul(mix, attended).astype(BF),
        ],
        axis=1,
    )

    def mine(part):
        return lax.dynamic_slice_in_dim(part, head_index * half, half, 0)

    def theirs(part):
        return lax.dynamic_slice_in_dim(part, (1 - head_index) * half, half, 0)

    far_sum = mine(part_far) + swap(theirs(part_far))
    from_far = partner(far_sum.astype(BF), "stream", 0).astype(F32)
    in_half = mine(grad_one) + (mine(part_h) + swap(theirs(part_h))) + from_far
    in_other = swap(in_half)
    grad_input = jnp.where(
        head_index == 0,
        jnp.concatenate([in_half, in_other], axis=0),
        jnp.concatenate([in_other, in_half], axis=0),
    )

    cross_red = scatter_both(cross_grad)
    kv_red = scatter_both(kv_grad.astype(BF))
    self_red = scatter_both(self_grad)

    dot_w = jnp.sum(kv_grad * kv_all.astype(F32), axis=1)
    feat_shift_grad = jnp.sum(
        kv_all.astype(F32) * jnp.concatenate([sums_cross[1], sums_cross[2]])[None], axis=1
    )
    feat_gain_grad = (dot_w - feat_shift * feat_shift_grad) / feat_gain

    bias_q_sum, _, bias_v_sum = (sums_self[0, one] for one in three)
    bias_v_sum = bias_v_sum + sums_self[1, three[2]]
    self_bias_grad = jnp.stack(
        [
            spread(bias_q_sum, col_start, width),
            spread(bias_v_sum, col_start, width),
            lead_mask * sums_one[2],
        ]
    )
    cross_bias_grad = jnp.stack(
        [
            spread(sums_cross[0], col_start, width),
            spread(sums_cross[2], col_start, width),
            lead_mask * sums_two[2],
        ]
    )
    gains_grad = lead_mask * jnp.stack(
        [sums_one[0], sums_two[0], query_mask * sums_three[0], text_mask * sums_three[0]]
    )
    shifts_grad = lead_mask * jnp.stack(
        [sums_one[1], sums_two[1], query_mask * sums_three[1], text_mask * sums_three[1]]
    )
    bias_in_full = spread(sum_pre[0], hidden_start, ffn_bias_in.shape[1])
    ffn_bias_in_grad = jnp.stack([query_mask * bias_in_full, text_mask * bias_in_full])
    ffn_bias_out_grad = lead_mask * jnp.stack(
        [query_mask * sums_three[2], text_mask * sums_three[2]]
    )
    (
        self_bias_sum,
        cross_bias_sum,
        gains_sum,
        shifts_sum,
        feat_gain_sum,
        feat_shift_sum,
        bias_in_sum,
        bias_out_sum,
    ) = all_totals(
        (
            self_bias_grad,
            cross_bias_grad,
            gains_grad,
            shifts_grad,
            feat_gain_grad,
            feat_shift_grad,
            ffn_bias_in_grad,
            ffn_bias_out_grad,
        )
    )
    return (
        output.reshape(items, 1, each, width),
        grad_input.reshape(items, 1, each, width),
        jnp.stack([self_red[:, one] for one in three]),
        self_bias_sum,
        self_red[:, 3 * cols :].T,
        cross_red[:, three[0]],
        jnp.stack([kv_red[:, one] for one in three[:2]]),
        cross_bias_sum,
        cross_red[:, three[1]].T,
        gains_sum,
        shifts_sum,
        feat_gain_sum,
        feat_shift_sum,
        ffn_red[:, :hidden_cols][None],
        bias_in_sum,
        ffn_red[:, hidden_cols:].T[None],
        bias_out_sum,
    )

def solution(mesh):
    placed = (
        P("items", "stream", None, None),
        P("items", None, None),
        P("items", None),
        P("items"),
        P(None, ("items", "stream"), "heads"),
        P(),
        P("heads", ("items", "stream")),
        P(("items", "stream"), "heads"),
        P(None, ("items", "stream"), "heads"),
        P(),
        P("heads", ("items", "stream")),
        P(),
        P(),
        P(),
        P(),
        P("stream", "items", "heads"),
        P(),
        P("stream", "heads", "items"),
        P(),
        P("items", "stream", None, None),
    )
    return jax.shard_map(
        body,
        mesh=mesh,
        in_specs=placed,
        out_specs=(
            P("items", "stream", None, None),
            P("items", "stream", None, None),
            P(None, ("items", "stream"), "heads"),
            P(),
            P("heads", ("items", "stream")),
            P(("items", "stream"), "heads"),
            P(None, ("items", "stream"), "heads"),
            P(),
            P("heads", ("items", "stream")),
            P(),
            P(),
            P(),
            P(),
            P("stream", "items", "heads"),
            P(),
            P("stream", "heads", "items"),
            P(),
        ),
        check_vma=False,
    )
```

time: 701 us -> 510 us (0.73)
  Pallas kernels: 0 us -> 116 us
  matrix products: 149 us -> 42.6 us
  other arithmetic: 119 us -> 32.1 us
  local copies, waits for them, and re-layouts: 129 us -> 67 us
  waiting for transfers between devices: 141 us -> 106 us
  starting transfers between devices: 109 us -> 94.9 us
    pallas_call x0 -> x8, Pallas kernels: none -> 116 us  [the longest x1 22.9 us: cross_back(): call(kernel, items // batch, [pl.BlockSpec(memory_space=pltpu.SMEM)] + [w...]
    dot_general x43 -> x10, matrix products: 149 us -> 42.6 us  [the longest x9 26.9 us: t_mul(): lax.dot_general(left, right, (((0,), (0,)), ((), ())), preferred_element_...]
    reduce_sum x23 -> x0, other arithmetic: 54.6 us -> none  [the longest x7 23.1 us: standard(): center = inputs - jnp.mean(inputs, axis=-1, keepdims=True)]
    convert_element_type x17 -> x3, local copies, waits for them, and re-layouts: 24 us -> 0.09 us  [scatter_items(): (own if up is None else own + up).astype(BF)]
    convert_element_type x21 -> x15, other arithmetic: 32.4 us -> 9.32 us  [the longest x9 4.01 us: scatter_items(): (own if up is None else own + up).astype(BF)]
    ppermute x42, waiting for transfers between devices: 84.7 us -> 65.3 us  [shift_ring(): lax.ppermute(shard, 'items', [(order[i], order[(i + step) % count]) for i...]
    concatenate x6 -> x3, local copies, waits for them, and re-layouts: 19.3 us -> 3.48 us  [the longest x1 2.83 us: body(): jnp.concatenate([t_mul(own, grad_near[:, :cols]).astype(BF), (t_mul(own,...]
    ppermute x21 -> x22, waiting for transfers between devices: 56.5 us -> 40.9 us  [partner(): lax.ppermute(shard, axis, [(i, i ^ 1 << distance) for i in range(lax.axis...]
  transfers between devices with their start and end apart: 65 -> 66, of which waited for: 30 -> 28; matrix products, arithmetic and copies ran while one was open for 32% -> 26% of each run, Pallas kernels for 0% -> 18%
where the time goes in v2:
time: 510 us; the launch traced here: 502 us
  Pallas kernels  116 us (23%)
  waiting for transfers between devices  106 us (21%)
  starting transfers between devices  94.9 us (19%)
  local copies, waits for them, and re-layouts  67 us (13%)
  matrix products  42.6 us (8%)
  between operations  42.4 us (8%)
  other arithmetic  32.1 us (6%)
    ppermute x42, starting transfers between devices, shift_ring(): lax.ppermute(shard, 'items', [(order[i], order[(i + step) % count]) for i...  80.8 us
    ppermute x42, waiting for transfers between devices, shift_ring(): lax.ppermute(shard, 'items', [(order[i], order[(i + step) % count]) for i...  65.3 us
    ppermute x22, waiting for transfers between devices, partner(): lax.ppermute(shard, axis, [(i, i ^ 1 << distance) for i in range(lax.axis...  40.9 us
    unnamed x98, local copies, waits for them, and re-layouts  27.9 us
    dot_general x9, matrix products, t_mul(): lax.dot_general(left, right, (((0,), (0,)), ((), ())), preferred_element_...  26.9 us
    pallas_call x1, Pallas kernels, cross_back(): call(kernel, items // batch, [pl.BlockSpec(memory_space=pltpu.SMEM)] + [w...  22.9 us
    pallas_call x1, Pallas kernels, self_back(): call(kernel, items // batch, [whole((rows, width))] * 4 + [whole((rows, 1...  20.2 us
    pallas_call x1, Pallas kernels, feature_norm(): call(kernel, items, [block((1, patches, width)), whole((1, width)), whole...  17.2 us
  transfers between devices with their start and end apart: 66, of which 28 were waited for; matrix products, arithmetic and copies ran while one was open for 26% of the time, Pallas kernels for 18%

profile of v2, /device:TPU:0, one launch (start us, length us, event | category | flops | bytes accessed | tf_op | source)
XLA Modules:
  0.0 501.5 jit_solution(13077571080775851764)
XLA Ops:
  8.3 3.0 collective-permute-start.19
  36.0 11.5 %copy.54.feat = bf16[16,257,1408]{2,1,0:T(8,128)(2,1)} copy(bf16[16,257,1408]{2,0,1:T(8,128)(2,1)} %param.33) | data formatting | bytes 23158784 | tf_op args[1]
  52.2 17.2 %shard_map.433 = bf16[16,264,1408]{2,1,0:T(8,128)(2,1)} custom-call(bf16[16,257,1408]{2,1,0:T(8,128)(2,1)} %copy.54.feat, f32[1,1408]{1,0:T(1,128)} %reshape.291.gain, f32[1,1408]{1,0:T(1,128)} %reshape.292.shift), custom_call_target="tpu_custom_call" | custom-call | bytes 23158784 | tf_op jit(solution)/shard_map/pallas_call | solution.py:239
  75.0 8.4 %collective-permute-done.11 = bf16[96,1152]{1,0:T(8,128)(2,1)S(1)} collective-permute-done((bf16[96,1152]{1,0:T(8,128)(2,1)S(1)}, bf16[96,1152]{1,0:T(8,128)(2,1)S(1)}, u32[]{:S(2)}, u32[]{:S(2)}) %collective-permute-start.11) | collective-permute-done | bytes 221216 | tf_op jit(solution)/shard_map/ppermute | solution.py:33
  83.4 3.8 collective-permute-start.20
  87.2 5.1 %collective-permute-done.3 = bf16[96,1152]{1,0:T(8,128)(2,1)S(1)} collective-permute-done((bf16[96,1152]{1,0:T(8,128)(2,1)S(1)}, bf16[96,1152]{1,0:T(8,128)(2,1)S(1)}, u32[]{:S(2)}, u32[]{:S(2)}) %collective-permute-start.3) | collective-permute-done | bytes 221216 | tf_op jit(solution)/shard_map/ppermute | solution.py:33
  92.3 13.3 %collective-permute-start.21 = (bf16[176,768]{1,0:T(8,128)(2,1)S(1)}, bf16[176,768]{1,0:T(8,128)(2,1)S(1)}, u32[]{:S(2)}, u32[]{:S(2)}) collective-permute-start(bf16[176,768]{1,0:T(8,128)(2,1)S(1)} %get-tuple-element.136), channel_id=1, source_target_pairs={{0,4},{8,0},{16,8},{24,16},{28,24},{20,28},{12,20},{4,12},{1,5},{9... | collective-permute-start | bytes 811016 | tf_op jit(solution)/shard_map/ppermute | solution.py:33
  109.5 2.5 collective-permute-start.6
  113.7 2.5 collective-permute-start.22
  118.5 3.0 collective-permute-start.23
  124.3 2.5 collective-permute-start.7
  128.3 2.5 collective-permute-start.8
  133.7 3.0 collective-permute-start.25
  139.7 2.5 collective-permute-start.26
  142.2 2.9 collective-permute-done.17
  146.4 3.4 collective-permute-done.9
  151.1 5.3 %shard_map.431 = (bf16[512,384]{1,0:T(8,128)(2,1)}, bf16[512,768]{1,0:T(8,128)(2,1)}, bf16[512,768]{1,0:T(8,128)(2,1)}) custom-call(bf16[512,768]{1,0:T(8,128)(2,1)} %bitcast.160, bf16[512,768]{1,0:T(8,128)(2,1)} %maximum_select_fusion.1.far, bf16[768,1152]{1,0:T(8,128)(2,1)} %copy-done.4, f32[1,1152]{1,0:T(1,128)} %reshape.290.bias), custom_call_target="tpu_custom_call" | custom-call | flops 1509949440 | bytes 3342336 | tf_op jit(solution)/shard_map/pallas_call | solution.py:261
  156.4 9.6 %shard_map.432 = (bf16[512,384]{1,0:T(8,128)(2,1)}, f32[512,768]{1,0:T(8,128)}) custom-call(bf16[512,384]{1,0:T(8,128)(2,1)} %get-tuple-element.57.q, bf16[512,768]{1,0:T(8,128)(2,1)} %get-tuple-element.58.kv, bf16[512,768]{1,0:T(8,128)(2,1)} %get-tuple-element.59.kv_far, f32[16,32,64]{2,1,0:T(8,128)} %add_convert_fusion.12.allowed, ...), custom_call_target="tpu_custom_call" | custom-call | flops 905969664 | bytes 4325376 | tf_op jit(solution)/shard_map/pallas_call | solution.py:297
  166.0 15.7 %add_convert_fusion = bf16[4224,768]{1,0:T(8,128)(2,1)} fusion(bf16[4224,1408]{1,0:T(8,128)(2,1)} %bitcast.144, bf16[1408,768]{1,0:T(8,128)(2,1)S(1)} %constant_dynamic-update-slice_fusion.18, f32[768]{0:T(1024)S(1)} %concatenate.79), kind=kOutput, calls=%fused_computation | convolution fusion | flops 9141682176 | bytes 20548608 | tf_op jit(solution)/shard_map/dot_general | solution.py:128
  182.9 16.2 %shard_map.434 = (f32[512,768]{1,0:T(8,128)}, f32[512,1]{1,0:T(8,128)}, bf16[512,768]{1,0:T(8,128)(2,1)}, bf16[512,384]{1,0:T(8,128)(2,1)}, bf16[512,384]{1,0:T(8,128)(2,1)}, /*index=5*/f32[512,768]{1,0:T(8,128)}) custom-call(bf16[512,768]{1,0:T(8,128)(2,1)} %bitcast.161, f32[512,768]{1,0:T(8,128)} %get-tuple-element.60.near, f32[512,768]{1,0:T(8,128)} %copy-done.16, ...), custom_call_target="tpu_custom_call" | custom-call | flops 1245708288 | bytes 14352384 | tf_op jit(solution)/shard_map/pallas_call | solution.py:351
  201.0 4.8 fusion.10
  206.9 11.9 %shard_map.435 = (f32[512,768]{1,0:T(8,128)}, bf16[512,768]{1,0:T(8,128)(2,1)}, f32[512,768]{1,0:T(8,128)}, f32[512,1]{1,0:T(8,128)}, bf16[512,1536]{1,0:T(8,128...) custom-call(s32[1]{0:T(128)} %bitcast.flag, f32[512,768]{1,0:T(8,128)} %get-tuple-element.61.unit, ...), custom_call_target="tpu_custom_call" | custom-call | flops 2415919104 | bytes 19660800 | tf_op jit(solution)/shard_map/pallas_call | solution.py:403
  231.0 12.9 %shard_map.436 = (bf16[512,768]{1,0:T(8,128)(2,1)}, f32[512,768]{1,0:T(8,128)}, bf16[512,768]{1,0:T(8,128)(2,1)}, bf16[512,1536]{1,0:T(8,128)(2,1)}, f32[512,768...) custom-call(f32[512,768]{1,0:T(8,128)} %get-tuple-element.63.z, f32[512,768]{1,0:T(8,128)} %get-tuple-element.64.near, ...), custom_call_target="tpu_custom_call" | custom-call | flops 2415919104 | bytes 20447232 | tf_op jit(solution)/shard_map/pallas_call | solution.py:458
  244.5 3.0 convolution_convert_fusion.1
  248.9 2.8 pad_maximum_fusion
  254.2 22.9 %shard_map.437 = (f32[512,768]{1,0:T(8,128)}, bf16[512,768]{1,0:T(8,128)(2,1)}, bf16[512,384]{1,0:T(8,128)(2,1)}, bf16[16,264,768]{2,1,0:T(8,128)(2,1)}, f32[512...) custom-call(s32[1]{0:T(128)} %bitcast.flag, f32[512,768]{1,0:T(8,128)} %get-tuple-element.67.grad_v, ...), custom_call_target="tpu_custom_call" | custom-call | flops 3114270720 | bytes 23199744 | tf_op jit(solution)/shard_map/pallas_call | solution.py:540
  282.4 16.6 %fusion.1 = (f32[1408]{0:T(1024)S(1)}, f32[1408]{0:T(1024)S(1)}, bf16[1408,768,1]{1,0,2:T(8,128)(2,1)S(1)}) fusion(bf16[1408,768]{1,0:T(8,128)(2,1)} %copy-done.7, f32[768]{0:T(1024)S(1)} %pad_maximum_fusion.12, bf16[16,264,1408]{2,1,0:T(8,128)(2,1)} %shard_map.433, bf16[16,264,768]{2,1,0:T(8,128)(2,1)} %get-tuple-element.87), kind=kOutput, calls=%fused_computation.5 | convolution fusion | flops 9141680128 | bytes 22722560 | tf_op jit(solution)/shard_map/dot_general | solution.py:136
  302.9 3.5 collective-permute-done.49
  309.2 2.9 collective-permute-done.50
  312.3 5.6 %collective-permute-done.51 = bf16[48,768]{1,0:T(8,128)(2,1)S(1)} collective-permute-done((bf16[48,768]{1,0:T(8,128)(2,1)S(1)}, bf16[48,768]{1,0:T(8,128)(2,1)S(1)}, u32[]{:S(2)}, u32[]{:S(2)}) %collective-permute-start.51) | collective-permute-done | bytes 73760 | tf_op jit(solution)/shard_map/ppermute | solution.py:33
  320.0 4.7 collective-permute-done.56
  328.8 5.5 %collective-permute-done.57 = bf16[88,768]{1,0:T(8,128)(2,1)S(1)} collective-permute-done((bf16[88,768]{1,0:T(8,128)(2,1)S(1)}, bf16[88,768]{1,0:T(8,128)(2,1)S(1)}, u32[]{:S(2)}, u32[]{:S(2)}) %collective-permute-start.57) | collective-permute-done | bytes 135200 | tf_op jit(solution)/shard_map/ppermute | solution.py:33
  334.3 3.2 collective-permute-start.58
  337.5 2.7 collective-permute-start.61
  340.2 3.8 collective-permute-done.58
  344.0 6.2 %collective-permute-start.59 = (bf16[88,768]{1,0:T(8,128)(2,1)S(1)}, bf16[88,768]{1,0:T(8,128)(2,1)S(1)}, u32[]{:S(2)}, u32[]{:S(2)}) collective-permute-start(bf16[88,768]{1,0:T(8,128)(2,1)S(1)} %add_convert_fusion.10), channel_id=1, source_target_pairs={{0,8},{8,16},{16,24},{24,28},{28,20},{20,12},{12,4},{4,0},{1,9},{9... | collective-permute-start | bytes 405512 | tf_op jit(solution)/shard_map/ppermute | solution.py:33
  351.0 4.7 collective-permute-done.59
  356.4 2.8 collective-permute-start.62
  359.2 20.2 %shard_map.438 = (f32[512,768]{1,0:T(8,128)}, bf16[512,768]{1,0:T(8,128)(2,1)}, bf16[512,1152]{1,0:T(8,128)(2,1)}, bf16[512,768]{1,0:T(8,128)(2,1)}, f32[512,768...) custom-call(f32[512,768]{1,0:T(8,128)} %get-tuple-element.72.after, ...), custom_call_target="tpu_custom_call" | custom-call | flops 2717908992 | bytes 16515072 | tf_op jit(solution)/shard_map/pallas_call | solution.py:629
  398.5 2.8 copy.55
  409.1 23.8 %collective-permute-done.44 = f32[166,128]{1,0:T(8,128)S(1)} collective-permute-done((f32[166,128]{1,0:T(8,128)S(1)}, f32[166,128]{1,0:T(8,128)S(1)}, u32[]{:S(2)}, u32[]{:S(2)}) %collective-permute-start.44) | collective-permute-done | bytes 85024 | tf_op jit(solution)/shard_map/ppermute | solution.py:18
  440.5 4.4 collective-permute-done.46
  446.9 4.1 collective-permute-done.47
  456.9 4.0 collective-permute-done.36
  470.9 3.5 collective-permute-done.38
  475.5 2.5 collective-permute-start.41
  481.7 2.5 collective-permute-start.42
  484.2 2.9 collective-permute-done.33
  (347 shorter events, 134.2 us)
Async XLA Ops:
  7.2 193.8 %all-gather.2.cloned.1.call-start = ((), (), s32[]{:S(2)}) async-start(), calls=%async_computation.1 | async-start | bytes 5308416 | tf_op jit(solution)/shard_map/all_gather | solution.py:730
  8.3 66.4 %collective-permute-start.19 = (bf16[88,768]{1,0:T(8,128)(2,1)S(1)}, bf16[88,768]{1,0:T(8,128)(2,1)S(1)}, u32[]{:S(2)}, u32[]{:S(2)}) collective-permute-start(bf16[88,768]{1,0:T(8,128)(2,1)S(1)} %pad_maximum_fusion.6), channel_id=1, source_target_pairs={{0,2},{2,0},{1,3},{3,1},{4,6},{6,4},{5,7},{7,5},{8,10},{10,8},{9,1... | collective-permute-start | bytes 405512 | tf_op jit(solution)/shard_map/ppermute | solution.py:18
  12.2 57.8 %collective-permute-start.10 = (bf16[48,1152]{1,0:T(8,128)(2,1)S(1)}, bf16[48,1152]{1,0:T(8,128)(2,1)S(1)}, u32[]{:S(2)}, u32[]{:S(2)}) collective-permute-start(bf16[48,1152]{1,0:T(8,128)(2,1)S(1)} %pad_maximum_fusion.8), channel_id=1, source_target_pairs={{0,2},{2,0},{1,3},{3,1},{4,6},{6,4},{5,7},{7,5},{8,10},{10,8},{9,1... | collective-permute-start | bytes 331784 | tf_op jit(solution)/shard_map/ppermute | solution.py:18
  13.1 59.4 %collective-permute-start.2 = (bf16[48,1152]{1,0:T(8,128)(2,1)S(1)}, bf16[48,1152]{1,0:T(8,128)(2,1)S(1)}, u32[]{:S(2)}, u32[]{:S(2)}) collective-permute-start(bf16[48,1152]{1,0:T(8,128)(2,1)S(1)} %pad_maximum_fusion.7), channel_id=1, source_target_pairs={{0,2},{2,0},{1,3},{3,1},{4,6},{6,4},{5,7},{7,5},{8,10},{10,8},{9,1... | collective-permute-start | bytes 331784 | tf_op jit(solution)/shard_map/ppermute | solution.py:18
  16.2 93.3 %collective-permute-start = (bf16[256,768]{1,0:T(8,128)(2,1)S(1)}, bf16[256,768]{1,0:T(8,128)(2,1)S(1)}, u32[]{:S(2)}, u32[]{:S(2)}) collective-permute-start(bf16[256,768]{1,0:T(8,128)(2,1)S(1)} %constant_dynamic-slice_fusion.9), channel_id=1, source_target_pairs={{0,2},{2,0},{1,3},{3,1},{4,6},{6,4},{5,7},{7,5},{8,10},{10,8},{9,1... | collective-permute-start | bytes 1179656 | tf_op jit(solution)/shard_map/ppermute | solution.py:18
  17.2 475.0 %reduce-scatter.2.cloned.1.call-start = ((), (), s32[]{:S(2)}) async-start(), calls=%async_computation.2 | async-start | bytes 5308416 | tf_op jit(solution)/shard_map/reduce_scatter | solution.py:804
  70.3 13.2 %collective-permute-start.11 = (bf16[96,1152]{1,0:T(8,128)(2,1)S(1)}, bf16[96,1152]{1,0:T(8,128)(2,1)S(1)}, u32[]{:S(2)}, u32[]{:S(2)}) collective-permute-start(bf16[96,1152]{1,0:T(8,128)(2,1)S(1)} %get-tuple-element.138), channel_id=1, source_target_pairs={{0,8},{8,16},{16,24},{24,28},{28,20},{20,12},{12,4},{4,0},{1,9},{9... | collective-permute-start | bytes 663560 | tf_op jit(solution)/shard_map/ppermute | solution.py:33
  72.4 33.2 %collective-permute-start.12 = (bf16[96,1152]{1,0:T(8,128)(2,1)S(1)}, bf16[96,1152]{1,0:T(8,128)(2,1)S(1)}, u32[]{:S(2)}, u32[]{:S(2)}) collective-permute-start(bf16[96,1152]{1,0:T(8,128)(2,1)S(1)} %get-tuple-element.138), channel_id=1, source_target_pairs={{0,4},{8,0},{16,8},{24,16},{28,24},{20,28},{12,20},{4,12},{1,5},{9... | collective-permute-start | bytes 663560 | tf_op jit(solution)/shard_map/ppermute | solution.py:33
  72.7 19.6 %collective-permute-start.3 = (bf16[96,1152]{1,0:T(8,128)(2,1)S(1)}, bf16[96,1152]{1,0:T(8,128)(2,1)S(1)}, u32[]{:S(2)}, u32[]{:S(2)}) collective-permute-start(bf16[96,1152]{1,0:T(8,128)(2,1)S(1)} %get-tuple-element.140), channel_id=1, source_target_pairs={{0,8},{8,16},{16,24},{24,28},{28,20},{20,12},{12,4},{4,0},{1,9},{9... | collective-permute-start | bytes 663560 | tf_op jit(solution)/shard_map/ppermute | solution.py:33
  74.7 31.0 %collective-permute-start.4 = (bf16[96,1152]{1,0:T(8,128)(2,1)S(1)}, bf16[96,1152]{1,0:T(8,128)(2,1)S(1)}, u32[]{:S(2)}, u32[]{:S(2)}) collective-permute-start(bf16[96,1152]{1,0:T(8,128)(2,1)S(1)} %get-tuple-element.140), channel_id=1, source_target_pairs={{0,4},{8,0},{16,8},{24,16},{28,24},{20,28},{12,20},{4,12},{1,5},{9... | collective-permute-start | bytes 663560 | tf_op jit(solution)/shard_map/ppermute | solution.py:33
  83.4 24.3 %collective-permute-start.20 = (bf16[176,768]{1,0:T(8,128)(2,1)S(1)}, bf16[176,768]{1,0:T(8,128)(2,1)S(1)}, u32[]{:S(2)}, u32[]{:S(2)}) collective-permute-start(bf16[176,768]{1,0:T(8,128)(2,1)S(1)} %get-tuple-element.136), channel_id=1, source_target_pairs={{0,8},{8,16},{16,24},{24,28},{28,20},{20,12},{12,4},{4,0},{1,9},{9... | collective-permute-start | bytes 811016 | tf_op jit(solution)/shard_map/ppermute | solution.py:33
  92.3 20.1 %collective-permute-start.21 = (bf16[176,768]{1,0:T(8,128)(2,1)S(1)}, bf16[176,768]{1,0:T(8,128)(2,1)S(1)}, u32[]{:S(2)}, u32[]{:S(2)}) collective-permute-start(bf16[176,768]{1,0:T(8,128)(2,1)S(1)} %get-tuple-element.136), channel_id=1, source_target_pairs={{0,4},{8,0},{16,8},{24,16},{28,24},{20,28},{12,20},{4,12},{1,5},{9... | collective-permute-start | bytes 811016 | tf_op jit(solution)/shard_map/ppermute | solution.py:33
  105.6 8.1 %collective-permute-start.13 = (bf16[96,1152]{1,0:T(8,128)(2,1)S(1)}, bf16[96,1152]{1,0:T(8,128)(2,1)S(1)}, u32[]{:S(2)}, u32[]{:S(2)}) collective-permute-start(bf16[96,1152]{1,0:T(8,128)(2,1)S(1)} %collective-permute-done.11), channel_id=1, source_target_pairs={{0,8},{8,16},{16,24},{24,28},{28,20},{20,12},{12,4},{4,0},{1,9},{9... | collective-permute-start | bytes 663560 | tf_op jit(solution)/shard_map/ppermute | solution.py:33
  105.7 15.8 %collective-permute-start.14 = (bf16[96,1152]{1,0:T(8,128)(2,1)S(1)}, bf16[96,1152]{1,0:T(8,128)(2,1)S(1)}, u32[]{:S(2)}, u32[]{:S(2)}) collective-permute-start(bf16[96,1152]{1,0:T(8,128)(2,1)S(1)} %collective-permute-done.12), channel_id=1, source_target_pairs={{0,4},{8,0},{16,8},{24,16},{28,24},{20,28},{12,20},{4,12},{1,5},{9... | collective-permute-start | bytes 663560 | tf_op jit(solution)/shard_map/ppermute | solution.py:33
  107.8 10.7 %collective-permute-start.5 = (bf16[96,1152]{1,0:T(8,128)(2,1)S(1)}, bf16[96,1152]{1,0:T(8,128)(2,1)S(1)}, u32[]{:S(2)}, u32[]{:S(2)}) collective-permute-start(bf16[96,1152]{1,0:T(8,128)(2,1)S(1)} %collective-permute-done.3), channel_id=1, source_target_pairs={{0,8},{8,16},{16,24},{24,28},{28,20},{20,12},{12,4},{4,0},{1,9},{9... | collective-permute-start | bytes 663560 | tf_op jit(solution)/shard_map/ppermute | solution.py:33
  109.5 12.1 %collective-permute-start.6 = (bf16[96,1152]{1,0:T(8,128)(2,1)S(1)}, bf16[96,1152]{1,0:T(8,128)(2,1)S(1)}, u32[]{:S(2)}, u32[]{:S(2)}) collective-permute-start(bf16[96,1152]{1,0:T(8,128)(2,1)S(1)} %collective-permute-done.4), channel_id=1, source_target_pairs={{0,4},{8,0},{16,8},{24,16},{28,24},{20,28},{12,20},{4,12},{1,5},{9... | collective-permute-start | bytes 663560 | tf_op jit(solution)/shard_map/ppermute | solution.py:33
  112.4 26.0 %collective-permute-start.1 = (bf16[256,768]{1,0:T(8,128)(2,1)S(1)}, bf16[256,768]{1,0:T(8,128)(2,1)S(1)}, u32[]{:S(2)}, u32[]{:S(2)}) collective-permute-start(bf16[256,768]{1,0:T(8,128)(2,1)S(1)} %collective-permute-done), channel_id=1, source_target_pairs={{0,1},{1,0},{2,3},{3,2},{4,5},{5,4},{6,7},{7,6},{8,9},{9,8},{10,11... | collective-permute-start | bytes 1179656 | tf_op jit(solution)/shard_map/ppermute | solution.py:18
  113.7 10.5 %collective-permute-start.22 = (bf16[176,768]{1,0:T(8,128)(2,1)S(1)}, bf16[176,768]{1,0:T(8,128)(2,1)S(1)}, u32[]{:S(2)}, u32[]{:S(2)}) collective-permute-start(bf16[176,768]{1,0:T(8,128)(2,1)S(1)} %collective-permute-done.20), channel_id=1, source_target_pairs={{0,8},{8,16},{16,24},{24,28},{28,20},{20,12},{12,4},{4,0},{1,9},{9... | collective-permute-start | bytes 811016 | tf_op jit(solution)/shard_map/ppermute | solution.py:33
  118.5 9.9 %collective-permute-start.23 = (bf16[176,768]{1,0:T(8,128)(2,1)S(1)}, bf16[176,768]{1,0:T(8,128)(2,1)S(1)}, u32[]{:S(2)}, u32[]{:S(2)}) collective-permute-start(bf16[176,768]{1,0:T(8,128)(2,1)S(1)} %collective-permute-done.21), channel_id=1, source_target_pairs={{0,4},{8,0},{16,8},{24,16},{28,24},{20,28},{12,20},{4,12},{1,5},{9... | collective-permute-start | bytes 811016 | tf_op jit(solution)/shard_map/ppermute | solution.py:33
  121.5 9.3 %collective-permute-start.15 = (bf16[96,1152]{1,0:T(8,128)(2,1)S(1)}, bf16[96,1152]{1,0:T(8,128)(2,1)S(1)}, u32[]{:S(2)}, u32[]{:S(2)}) collective-permute-start(bf16[96,1152]{1,0:T(8,128)(2,1)S(1)} %collective-permute-done.13), channel_id=1, source_target_pairs={{0,8},{8,16},{16,24},{24,28},{28,20},{20,12},{12,4},{4,0},{1,9},{9... | collective-permute-start | bytes 663560 | tf_op jit(solution)/shard_map/ppermute | solution.py:33
  121.6 15.2 %collective-permute-start.16 = (bf16[96,1152]{1,0:T(8,128)(2,1)S(1)}, bf16[96,1152]{1,0:T(8,128)(2,1)S(1)}, u32[]{:S(2)}, u32[]{:S(2)}) collective-permute-start(bf16[96,1152]{1,0:T(8,128)(2,1)S(1)} %collective-permute-done.14), channel_id=1, source_target_pairs={{0,4},{8,0},{16,8},{24,16},{28,24},{20,28},{12,20},{4,12},{1,5},{9... | collective-permute-start | bytes 663560 | tf_op jit(solution)/shard_map/ppermute | solution.py:33
  124.3 9.5 %collective-permute-start.7 = (bf16[96,1152]{1,0:T(8,128)(2,1)S(1)}, bf16[96,1152]{1,0:T(8,128)(2,1)S(1)}, u32[]{:S(2)}, u32[]{:S(2)}) collective-permute-start(bf16[96,1152]{1,0:T(8,128)(2,1)S(1)} %collective-permute-done.5), channel_id=1, source_target_pairs={{0,8},{8,16},{16,24},{24,28},{28,20},{20,12},{12,4},{4,0},{1,9},{9... | collective-permute-start | bytes 663560 | tf_op jit(solution)/shard_map/ppermute | solution.py:33
  128.3 8.5 %collective-permute-start.8 = (bf16[96,1152]{1,0:T(8,128)(2,1)S(1)}, bf16[96,1152]{1,0:T(8,128)(2,1)S(1)}, u32[]{:S(2)}, u32[]{:S(2)}) collective-permute-start(bf16[96,1152]{1,0:T(8,128)(2,1)S(1)} %collective-permute-done.6), channel_id=1, source_target_pairs={{0,4},{8,0},{16,8},{24,16},{28,24},{20,28},{12,20},{4,12},{1,5},{9... | collective-permute-start | bytes 663560 | tf_op jit(solution)/shard_map/ppermute | solution.py:33
  130.8 8.8 %collective-permute-start.24 = (bf16[176,768]{1,0:T(8,128)(2,1)S(1)}, bf16[176,768]{1,0:T(8,128)(2,1)S(1)}, u32[]{:S(2)}, u32[]{:S(2)}) collective-permute-start(bf16[176,768]{1,0:T(8,128)(2,1)S(1)} %collective-permute-done.22), channel_id=1, source_target_pairs={{0,8},{8,16},{16,24},{24,28},{28,20},{20,12},{12,4},{4,0},{1,9},{9... | collective-permute-start | bytes 811016 | tf_op jit(solution)/shard_map/ppermute | solution.py:33
  133.7 8.5 %collective-permute-start.25 = (bf16[176,768]{1,0:T(8,128)(2,1)S(1)}, bf16[176,768]{1,0:T(8,128)(2,1)S(1)}, u32[]{:S(2)}, u32[]{:S(2)}) collective-permute-start(bf16[176,768]{1,0:T(8,128)(2,1)S(1)} %collective-permute-done.23), channel_id=1, source_target_pairs={{0,4},{8,0},{16,8},{24,16},{28,24},{20,28},{12,20},{4,12},{1,5},{9... | collective-permute-start | bytes 811016 | tf_op jit(solution)/shard_map/ppermute | solution.py:33
  136.8 8.4 %collective-permute-start.17 = (bf16[96,1152]{1,0:T(8,128)(2,1)S(1)}, bf16[96,1152]{1,0:T(8,128)(2,1)S(1)}, u32[]{:S(2)}, u32[]{:S(2)}) collective-permute-start(bf16[96,1152]{1,0:T(8,128)(2,1)S(1)} %collective-permute-done.15), channel_id=1, source_target_pairs={{0,8},{8,16},{16,24},{24,28},{28,20},{20,12},{12,4},{4,0},{1,9},{9... | collective-permute-start | bytes 663560 | tf_op jit(solution)/shard_map/ppermute | solution.py:33
  136.9 13.0 %collective-permute-start.9 = (bf16[96,1152]{1,0:T(8,128)(2,1)S(1)}, bf16[96,1152]{1,0:T(8,128)(2,1)S(1)}, u32[]{:S(2)}, u32[]{:S(2)}) collective-permute-start(bf16[96,1152]{1,0:T(8,128)(2,1)S(1)} %collective-permute-done.7), channel_id=1, source_target_pairs={{0,8},{8,16},{16,24},{24,28},{28,20},{20,12},{12,4},{4,0},{1,9},{9... | collective-permute-start | bytes 663560 | tf_op jit(solution)/shard_map/ppermute | solution.py:33
  139.7 26.3 %collective-permute-start.26 = (bf16[176,768]{1,0:T(8,128)(2,1)S(1)}, bf16[176,768]{1,0:T(8,128)(2,1)S(1)}, u32[]{:S(2)}, u32[]{:S(2)}) collective-permute-start(bf16[176,768]{1,0:T(8,128)(2,1)S(1)} %collective-permute-done.24), channel_id=1, source_target_pairs={{0,8},{8,16},{16,24},{24,28},{28,20},{20,12},{12,4},{4,0},{1,9},{9... | collective-permute-start | bytes 811016 | tf_op jit(solution)/shard_map/ppermute | solution.py:33
  166.0 15.7 %collective-permute-start.18 = (f32[512,768]{1,0:T(8,128)}, f32[512,768]{1,0:T(8,128)S(1)}, u32[]{:S(2)}, u32[]{:S(2)}) collective-permute-start(f32[512,768]{1,0:T(8,128)} %get-tuple-element.60.near), channel_id=1, source_target_pairs={{0,1},{1,0},{2,3},{3,2},{4,5},{5,4},{6,7},{7,6},{8,9},{9,8},{10,11... | collective-permute-start | bytes 4718600 | tf_op jit(solution)/shard_map/ppermute | solution.py:18
  218.8 11.0 %collective-permute-start.28 = (f32[512,768]{1,0:T(8,128)}, f32[512,768]{1,0:T(8,128)S(1)}, u32[]{:S(2)}, u32[]{:S(2)}) collective-permute-start(f32[512,768]{1,0:T(8,128)} %get-tuple-element.64.near), channel_id=1, source_target_pairs={{0,1},{1,0},{2,3},{3,2},{4,5},{5,4},{6,7},{7,6},{8,9},{9,8},{10,11... | collective-permute-start | bytes 4718600 | tf_op jit(solution)/shard_map/ppermute | solution.py:18
  243.9 9.1 %collective-permute-start.29 = (f32[512,768]{1,0:T(8,128)}, f32[512,768]{1,0:T(8,128)S(1)}, u32[]{:S(2)}, u32[]{:S(2)}) collective-permute-start(f32[512,768]{1,0:T(8,128)} %get-tuple-element.68.near), channel_id=1, source_target_pairs={{0,1},{1,0},{2,3},{3,2},{4,5},{5,4},{6,7},{7,6},{8,9},{9,8},{10,11... | collective-permute-start | bytes 4718600 | tf_op jit(solution)/shard_map/ppermute | solution.py:18
  280.1 19.7 %collective-permute-start.48 = (bf16[8,48,768]{2,1,0:T(8,128)(2,1)S(1)}, bf16[8,48,768]{2,1,0:T(8,128)(2,1)S(1)}, u32[]{:S(2)}, u32[]{:S(2)}) collective-permute-start(bf16[8,48,768]{2,1,0:T(8,128)(2,1)S(1)} %dynamic-slice_bitcast_fusion.2), channel_id=1, source_target_pairs={{0,2},{2,0},{1,3},{3,1},{4,6},{6,4},{5,7},{7,5},{8,10},{10,8},{9,1... | collective-permute-start | bytes 1769480 | tf_op jit(solution)/shard_map/ppermute | solution.py:18
  299.1 25.5 %collective-permute-start.56 = (bf16[8,88,768]{2,1,0:T(8,128)(2,1)S(1)}, bf16[8,88,768]{2,1,0:T(8,128)(2,1)}, u32[]{:S(2)}, u32[]{:S(2)}) collective-permute-start(bf16[8,88,768]{2,1,0:T(8,128)(2,1)S(1)} %dynamic-slice_bitcast_fusion.1), channel_id=1, source_target_pairs={{0,2},{2,0},{1,3},{3,1},{4,6},{6,4},{5,7},{7,5},{8,10},{10,8},{9,1... | collective-permute-start | bytes 3244040 | tf_op jit(solution)/shard_map/ppermute | solution.py:18
  299.8 59.5 %collective-permute-start.30 = (f32[512,768]{1,0:T(8,128)}, f32[512,768]{1,0:T(8,128)}, u32[]{:S(2)}, u32[]{:S(2)}) collective-permute-start(f32[512,768]{1,0:T(8,128)} %get-tuple-element.73.near), channel_id=1, source_target_pairs={{0,1},{1,0},{2,3},{3,2},{4,5},{5,4},{6,7},{7,6},{8,9},{9,8},{10,11... | collective-permute-start | bytes 4718600 | tf_op jit(solution)/shard_map/ppermute | solution.py:18
  317.9 10.3 %collective-permute-start.54 = (bf16[48,768]{1,0:T(8,128)(2,1)S(1)}, bf16[48,768]{1,0:T(8,128)(2,1)S(1)}, u32[]{:S(2)}, u32[]{:S(2)}) collective-permute-start(bf16[48,768]{1,0:T(8,128)(2,1)S(1)} %get-tuple-element.157), channel_id=1, source_target_pairs={{0,4},{8,0},{16,8},{24,16},{28,24},{20,28},{12,20},{4,12},{1,5},{9... | collective-permute-start | bytes 221192 | tf_op jit(solution)/shard_map/ppermute | solution.py:33
  318.0 19.5 %collective-permute-start.52 = (bf16[48,768]{1,0:T(8,128)(2,1)S(1)}, bf16[48,768]{1,0:T(8,128)(2,1)S(1)}, u32[]{:S(2)}, u32[]{:S(2)}) collective-permute-start(bf16[48,768]{1,0:T(8,128)(2,1)S(1)} %get-tuple-element.156), channel_id=1, source_target_pairs={{0,8},{8,16},{16,24},{24,28},{28,20},{20,12},{12,4},{4,0},{1,9},{9... | collective-permute-start | bytes 221192 | tf_op jit(solution)/shard_map/ppermute | solution.py:33
  328.2 9.2 %collective-permute-start.55 = (bf16[48,768]{1,0:T(8,128)(2,1)S(1)}, bf16[48,768]{1,0:T(8,128)(2,1)S(1)}, u32[]{:S(2)}, u32[]{:S(2)}) collective-permute-start(bf16[48,768]{1,0:T(8,128)(2,1)S(1)} %add_convert_fusion.13), channel_id=1, source_target_pairs={{0,4},{8,0},{16,8},{24,16},{28,24},{20,28},{12,20},{4,12},{1,5},{9... | collective-permute-start | bytes 221192 | tf_op jit(solution)/shard_map/ppermute | solution.py:33
  334.3 9.7 %collective-permute-start.58 = (bf16[88,768]{1,0:T(8,128)(2,1)S(1)}, bf16[88,768]{1,0:T(8,128)(2,1)S(1)}, u32[]{:S(2)}, u32[]{:S(2)}) collective-permute-start(bf16[88,768]{1,0:T(8,128)(2,1)S(1)} %add_convert_fusion.11), channel_id=1, source_target_pairs={{0,8},{8,16},{16,24},{24,28},{28,20},{20,12},{12,4},{4,0},{1,9},{9... | collective-permute-start | bytes 405512 | tf_op jit(solution)/shard_map/ppermute | solution.py:33
  337.5 13.5 %collective-permute-start.61 = (bf16[88,768]{1,0:T(8,128)(2,1)S(1)}, bf16[88,768]{1,0:T(8,128)(2,1)S(1)}, u32[]{:S(2)}, u32[]{:S(2)}) collective-permute-start(bf16[88,768]{1,0:T(8,128)(2,1)S(1)} %get-tuple-element.150), channel_id=1, source_target_pairs={{0,4},{8,0},{16,8},{24,16},{28,24},{20,28},{12,20},{4,12},{1,5},{9... | collective-permute-start | bytes 405512 | tf_op jit(solution)/shard_map/ppermute | solution.py:33
  344.0 11.6 %collective-permute-start.59 = (bf16[88,768]{1,0:T(8,128)(2,1)S(1)}, bf16[88,768]{1,0:T(8,128)(2,1)S(1)}, u32[]{:S(2)}, u32[]{:S(2)}) collective-permute-start(bf16[88,768]{1,0:T(8,128)(2,1)S(1)} %add_convert_fusion.10), channel_id=1, source_target_pairs={{0,8},{8,16},{16,24},{24,28},{28,20},{20,12},{12,4},{4,0},{1,9},{9... | collective-permute-start | bytes 405512 | tf_op jit(solution)/shard_map/ppermute | solution.py:33
  356.4 50.4 %collective-permute-start.62 = (bf16[88,768]{1,0:T(8,128)(2,1)}, bf16[88,768]{1,0:T(8,128)(2,1)}, u32[]{:S(2)}, u32[]{:S(2)}) collective-permute-start(bf16[88,768]{1,0:T(8,128)(2,1)} %get-tuple-element.148), channel_id=1, source_target_pairs={{0,4},{8,0},{16,8},{24,16},{28,24},{20,28},{12,20},{4,12},{1,5},{9... | collective-permute-start | bytes 405512 | tf_op jit(solution)/shard_map/ppermute | solution.py:33
  359.2 76.6 %collective-permute-start.60 = (bf16[88,768]{1,0:T(8,128)(2,1)}, bf16[88,768]{1,0:T(8,128)(2,1)}, u32[]{:S(2)}, u32[]{:S(2)}) collective-permute-start(bf16[88,768]{1,0:T(8,128)(2,1)} %get-tuple-element.147), channel_id=1, source_target_pairs={{0,8},{8,16},{16,24},{24,28},{28,20},{20,12},{12,4},{4,0},{1,9},{9... | collective-permute-start | bytes 405512 | tf_op jit(solution)/shard_map/ppermute | solution.py:33
  392.5 13.1 %collective-permute-start.43 = (f32[166,128]{1,0:T(8,128)}, f32[166,128]{1,0:T(8,128)}, u32[]{:S(2)}, u32[]{:S(2)}) collective-permute-start(f32[166,128]{1,0:T(8,128)} %bitcast.56), channel_id=1, source_target_pairs={{0,1},{1,0},{2,3},{3,2},{4,5},{5,4},{6,7},{7,6},{8,9},{9,8},{10,11... | collective-permute-start | bytes 254984 | tf_op jit(solution)/shard_map/ppermute | solution.py:18
  402.5 50.6 %collective-permute-start.35 = (bf16[8,48,1536]{2,1,0:T(8,128)(2,1)}, bf16[8,48,1536]{2,1,0:T(8,128)(2,1)S(1)}, u32[]{:S(2)}, u32[]{:S(2)}) collective-permute-start(bf16[8,48,1536]{2,1,0:T(8,128)(2,1)} %dynamic-slice_bitcast_fusion), channel_id=1, source_target_pairs={{0,2},{2,0},{1,3},{3,1},{4,6},{6,4},{5,7},{7,5},{8,10},{10,8},{9,1... | collective-permute-start | bytes 3538952 | tf_op jit(solution)/shard_map/ppermute | solution.py:18
  404.4 73.7 %collective-permute-start.32 = (f32[256,768]{1,0:T(8,128)}, f32[256,768]{1,0:T(8,128)}, u32[]{:S(2)}, u32[]{:S(2)}) collective-permute-start(f32[256,768]{1,0:T(8,128)} %constant_dynamic-slice_fusion.1), channel_id=1, source_target_pairs={{0,1},{1,0},{2,3},{3,2},{4,5},{5,4},{6,7},{7,6},{8,9},{9,8},{10,11... | collective-permute-start | bytes 2359304 | tf_op jit(solution)/shard_map/ppermute | solution.py:18
  405.6 78.6 %collective-permute-start.31 = (f32[256,768]{1,0:T(8,128)}, f32[256,768]{1,0:T(8,128)}, u32[]{:S(2)}, u32[]{:S(2)}) collective-permute-start(f32[256,768]{1,0:T(8,128)} %constant_dynamic-slice_fusion.2), channel_id=1, source_target_pairs={{0,1},{1,0},{2,3},{3,2},{4,5},{5,4},{6,7},{7,6},{8,9},{9,8},{10,11... | collective-permute-start | bytes 2359304 | tf_op jit(solution)/shard_map/ppermute | solution.py:18
  406.9 26.0 %collective-permute-start.44 = (f32[166,128]{1,0:T(8,128)S(1)}, f32[166,128]{1,0:T(8,128)S(1)}, u32[]{:S(2)}, u32[]{:S(2)}) collective-permute-start(f32[166,128]{1,0:T(8,128)S(1)} %bitcast_add_fusion.1), channel_id=1, source_target_pairs={{0,2},{2,0},{1,3},{3,1},{4,6},{6,4},{5,7},{7,5},{8,10},{10,8},{9,1... | collective-permute-start | bytes 254984 | tf_op jit(solution)/shard_map/ppermute | solution.py:18
  479.7 8.9 %collective-permute-start.39 = (bf16[48,1536]{1,0:T(8,128)(2,1)S(1)}, bf16[48,1536]{1,0:T(8,128)(2,1)S(1)}, u32[]{:S(2)}, u32[]{:S(2)}) collective-permute-start(bf16[48,1536]{1,0:T(8,128)(2,1)S(1)} %get-tuple-element.143), channel_id=1, source_target_pairs={{0,8},{8,16},{16,24},{24,28},{28,20},{20,12},{12,4},{4,0},{1,9},{9... | collective-permute-start | bytes 442376 | tf_op jit(solution)/shard_map/ppermute | solution.py:33
  (63 other events, 722.9 us)
Sparse Core Ops, SparseCore 0:
  17.3 94.5 all-gather.1
  251.8 103.7 reduce-scatter.1
